TPU v7x, 32 devices: a whole 2x2x4 slice. The times are simulated.
32 devices in a mesh: dp: 4 (over z), fsdp: 8 (over y, x, core).
Axes of the slice: x: 2, y: 2, z: 4, core: 2. Of those that a mesh axis runs over, the one named last changes fastest.
Arguments:
- inputs: bfloat16 [2, 20480, 768], P(None, ('dp', 'fsdp')), may hold values from -6 to 6
- cotangent: bfloat16 [2, 20480, 768], P(None, ('dp', 'fsdp')), may hold values from -6 to 6
- qkv_weight: bfloat16 [768, 2304], P(('dp', 'fsdp')), may hold values from -0.21875 to 0.21875
- proj_weight: bfloat16 [768, 768], P(('dp', 'fsdp')), may hold values from -1.5 to 1.5
- expand_weight: bfloat16 [768, 2304], P(('dp', 'fsdp')), may hold values from -0.21875 to 0.21875
- contract_weight: bfloat16 [1152, 768], P(None, ('dp', 'fsdp')), may hold values from -0.1875 to 0.1875
- prenorm: bfloat16 [768], P(('dp', 'fsdp')), may hold values from 0.5 to 1.5
- midnorm: bfloat16 [768], P(('dp', 'fsdp')), may hold values from 0.5 to 1.5
- lengths: int32 [2, 4, 8], P(None, 'dp'), may hold values from 1 to 20, as said below
- dealing: int32 [2, 160], P(None, ('dp', 'fsdp')), may hold values from 0 to 159, as said below
- holders: int32 [2, 2, 160], P(None, None, ('dp', 'fsdp')), may hold values from 0 to 5, as said below
- counts: int32 [2, 160], P(None, ('dp', 'fsdp')), may hold values from 1 to 128, as said below
Outputs:
- result: bfloat16 [2, 20480, 768], P(None, ('dp', 'fsdp'))
- input_grad: bfloat16 [2, 20480, 768], P(None, ('dp', 'fsdp'))
- grad_qkv: float32 [768, 2304], P(('dp', 'fsdp'))
- grad_proj: float32 [768, 768], P(('dp', 'fsdp'))
- grad_expand: float32 [768, 2304], P(('dp', 'fsdp'))
- grad_contract: float32 [1152, 768], P(None, ('dp', 'fsdp'))
- grad_prenorm: float32 [768], P(('dp', 'fsdp'))
- grad_midnorm: float32 [768], P(('dp', 'fsdp'))
Inputs may be any that keep to these rules, and one draw needn't show every extreme that they name: lengths[m, g] are the block counts of 8 sequences laid end to end over the 40 blocks of dp index g; they sum to 40 and one of them is 20. `dealing`: the 5 slots of device d hold a permutation of its own blocks, numbered in sequence order d * 5 to d * 5 + 4. holders[m, 0, s] is the slot number on the same device of block dealing[m, s] - 1, or 5 where dealing[m, s] is the device's first block in sequence order; holders[m, 1, s] is the slot number on the same device of block dealing[m, s] + 1, or 5 where dealing[m, s] is the device's last block in sequence order. counts[m, o] is 128 except for the last block of a sequence.
All inputs are finite; a program needn't handle non-finite values.
Results may differ from a plain program's by a relative error of at most 0.015.
Values may be sent and summed in bfloat16 or wider, within the bound.
A program may use at most 256 MiB of HBM per device.

v0:
```python
import jax
import jax.numpy as jnp
from jax import lax
from jax.sharding import PartitionSpec as P

HEAD_DIM = 64


norm_epsilon = 1e-05
rope_base = 10000.0
masked_score = -1e30


def shifted(block, axis, distance):
    devices = range(lax.axis_size(axis))
    route = [(i - distance, i) for i in devices if i - distance in devices]
    return lax.ppermute(block, axis, route)


def layer_norm(values, gains):
    centred = values - jnp.mean(values, axis=-1, keepdims=True)
    spread = jnp.mean(centred * centred, axis=-1, keepdims=True)
    return centred * lax.rsqrt(spread + norm_epsilon) * gains


def rotate_half(values):
    halfway = values.shape[-1] // 2
    return jnp.concatenate([-values[..., halfway:], values[..., :halfway]], axis=-1)


def rope_tables(positions, head_size):
    halfway = head_size // 2
    exponents = jnp.arange(halfway, dtype=jnp.float32) * (2.0 / head_size)
    frequency = rope_base ** (-exponents)
    angles = positions[:, None] * frequency[None, :]
    angles = jnp.concatenate([angles, angles], axis=-1)
    return (jnp.cos(angles)[:, None, :], jnp.sin(angles)[:, None, :])


def apply_rope(values, cos_table, sin_table):
    return values * cos_table + rotate_half(values) * sin_table


def rope_back(values, cos_table, sin_table):
    return values * cos_table - rotate_half(values * sin_table)


def geglu(expanded):
    halfway = expanded.shape[-1] // 2
    return jax.nn.gelu(expanded[:, :halfway], approximate=False) * expanded[:, halfway:]


def window_mask(has_prev, has_next, key_valid, block_rows):
    half_rows = block_rows // 2
    query_row = jnp.arange(block_rows)[:, None]
    key_col = jnp.arange(2 * block_rows)[None, :]
    relative = key_col - query_row
    inside = (relative >= 0) & (relative <= block_rows)
    before_ok = (key_col >= half_rows)[None] | has_prev[:, None, None]
    after_ok = (key_col < half_rows + block_rows)[None] | has_next[:, None, None]
    return (inside[None] & before_ok & after_ok & (key_valid[:, None, :] > 0))[:, None]


def slot_layout(dealt_blocks, seq_starts, seq_lasts, group_blocks, valid_rows, block_rows):
    within = dealt_blocks % group_blocks
    begin = jnp.max(jnp.where(seq_starts <= within[:, None], seq_starts, 0), axis=1)
    offset = within - begin
    is_last = jnp.any(seq_lasts == within[:, None], axis=1)
    row_ids = jnp.arange(block_rows)
    positions = (offset[:, None] * block_rows + row_ids[None, :]).reshape(-1).astype(jnp.float32)
    row_mask = (row_ids[None, :] < valid_rows[:, None]).astype(jnp.float32).reshape(-1, 1)
    return (offset > 0, jnp.logical_not(is_last), positions, row_mask)


def local(
    inputs,
    cotangent,
    qkv_weight,
    proj_weight,
    expand_weight,
    contract_weight,
    prenorm,
    midnorm,
    lengths,
    dealing,
    holders,
    counts,
):
    micro_count = inputs.shape[0]
    blocks_here = dealing.shape[1]
    row_count = inputs.shape[1]
    block_rows = row_count // blocks_here
    half_rows = block_rows // 2
    model_width = inputs.shape[2]
    head_size = HEAD_DIM
    head_count = model_width // head_size
    score_scale = head_size ** (-0.5)
    group_blocks = blocks_here * lax.axis_size("fsdp")
    grad_totals = None
    results = []
    input_grads = []
    for batch_idx in range(micro_count):
        full_fwd = (
            lax.all_gather(qkv_weight, ("dp", "fsdp"), axis=0, tiled=True),
            lax.all_gather(proj_weight, ("dp", "fsdp"), axis=0, tiled=True),
            lax.all_gather(expand_weight, ("dp", "fsdp"), axis=0, tiled=True),
            lax.all_gather(contract_weight, ("dp", "fsdp"), axis=1, tiled=True),
            lax.all_gather(prenorm, ("dp", "fsdp"), axis=0, tiled=True),
            lax.all_gather(midnorm, ("dp", "fsdp"), axis=0, tiled=True),
        )
        w_qkv, w_proj, w_expand, w_contract, gain_pre, gain_mid = full_fwd
        gain_pre = gain_pre.astype(jnp.float32)
        gain_mid = gain_mid.astype(jnp.float32)
        dealt_blocks = dealing[batch_idx]
        seq_blocks = lengths[batch_idx, 0]
        seq_ends = jnp.cumsum(seq_blocks)
        seq_starts = jnp.broadcast_to(
            (seq_ends - seq_blocks)[None, :], (blocks_here, seq_blocks.shape[0])
        )
        seq_lasts = jnp.broadcast_to((seq_ends - 1)[None, :], (blocks_here, seq_blocks.shape[0]))
        local_orig = dealt_blocks % blocks_here
        valid_rows = jnp.take(counts[batch_idx], local_orig)
        has_prev, has_next, positions, row_mask = slot_layout(
            dealt_blocks, seq_starts, seq_lasts, group_blocks, valid_rows, block_rows
        )
        cos_table, sin_table = rope_tables(positions, head_size)
        last_slot = jnp.sum(jnp.where(local_orig == blocks_here - 1, jnp.arange(blocks_here), 0))
        first_slot = jnp.sum(jnp.where(local_orig == 0, jnp.arange(blocks_here), 0))
        pred_slot = holders[batch_idx, 0]
        succ_slot = holders[batch_idx, 1]
        mask_blocks = row_mask.reshape(blocks_here, block_rows)
        x_rows = inputs[batch_idx].astype(jnp.float32)
        normed_one = layer_norm(x_rows, gain_pre).astype(jnp.bfloat16)
        qkv_full = jnp.dot(normed_one, w_qkv, preferred_element_type=jnp.float32).reshape(
            row_count, 3, head_count, head_size
        )
        query_rot = apply_rope(qkv_full[:, 0], cos_table, sin_table).astype(jnp.bfloat16)
        key_own = apply_rope(qkv_full[:, 1], cos_table, sin_table).astype(jnp.bfloat16)
        value_own = qkv_full[:, 2].astype(jnp.bfloat16)
        kv_local = jnp.stack(
            [
                key_own.reshape(blocks_here, block_rows, model_width),
                value_own.reshape(blocks_here, block_rows, model_width),
            ]
        )
        outgoing_prev = lax.dynamic_index_in_dim(kv_local, last_slot, axis=1, keepdims=False)[
            :, half_rows:
        ]
        incoming_prev = shifted(outgoing_prev, "fsdp", 1)
        outgoing_next = lax.dynamic_index_in_dim(kv_local, first_slot, axis=1, keepdims=False)[
            :, :half_rows
        ]
        outgoing_valid = lax.dynamic_index_in_dim(mask_blocks, first_slot, axis=0, keepdims=False)[
            :half_rows
        ].astype(jnp.bfloat16)
        incoming_next, incoming_valid = shifted((outgoing_next, outgoing_valid), "fsdp", -1)
        prev_all = jnp.concatenate([kv_local[:, :, half_rows:], incoming_prev[:, None]], axis=1)
        next_all = jnp.concatenate([kv_local[:, :, :half_rows], incoming_next[:, None]], axis=1)
        valid_all = jnp.concatenate(
            [mask_blocks[:, :half_rows], incoming_valid.astype(jnp.float32)[None]], axis=0
        )
        kv_pred = jnp.take(prev_all, pred_slot, axis=1)
        kv_succ = jnp.take(next_all, succ_slot, axis=1)
        key_valid = jnp.concatenate(
            [
                jnp.ones((blocks_here, half_rows), jnp.float32),
                mask_blocks,
                jnp.take(valid_all, succ_slot, axis=0),
            ],
            axis=1,
        )
        allowed = window_mask(has_prev, has_next, key_valid, block_rows)
        key_tiles = jnp.concatenate([kv_pred[0], kv_local[0], kv_succ[0]], axis=1).reshape(
            blocks_here, 2 * block_rows, head_count, head_size
        )
        value_tiles = jnp.concatenate([kv_pred[1], kv_local[1], kv_succ[1]], axis=1).reshape(
            blocks_here, 2 * block_rows, head_count, head_size
        )
        query_tiles = query_rot.reshape(blocks_here, block_rows, head_count, head_size)
        scores = (
            jnp.einsum(
                "brhe,bche->bhrc", query_tiles, key_tiles, preferred_element_type=jnp.float32
            )
            * score_scale
        )
        scores = jnp.where(allowed, scores, masked_score)
        row_top = jnp.max(scores, axis=-1, keepdims=True)
        lifted = jnp.exp(scores - row_top)
        row_total = jnp.sum(lifted, axis=-1, keepdims=True)
        attn_probs = lifted / row_total
        log_total = row_top + jnp.log(row_total)
        prob_low = attn_probs.astype(jnp.bfloat16)
        attended = jnp.einsum(
            "bhrc,bche->brhe", prob_low, value_tiles, preferred_element_type=jnp.float32
        )
        attended = attended.reshape(row_count, model_width).astype(jnp.bfloat16)
        attn_branch = jnp.dot(attended, w_proj, preferred_element_type=jnp.float32)
        mid_rows = x_rows + row_mask * attn_branch
        normed_two = layer_norm(mid_rows, gain_mid).astype(jnp.bfloat16)
        expanded = jnp.dot(normed_two, w_expand, preferred_element_type=jnp.float32)
        hidden = geglu(expanded).astype(jnp.bfloat16)
        ffn_branch = jnp.dot(hidden, w_contract, preferred_element_type=jnp.float32)
        results.append((mid_rows + row_mask * ffn_branch).astype(jnp.bfloat16))
        full_bwd = (
            lax.all_gather(qkv_weight, ("dp", "fsdp"), axis=0, tiled=True),
            lax.all_gather(proj_weight, ("dp", "fsdp"), axis=0, tiled=True),
            lax.all_gather(expand_weight, ("dp", "fsdp"), axis=0, tiled=True),
            lax.all_gather(contract_weight, ("dp", "fsdp"), axis=1, tiled=True),
            lax.all_gather(prenorm, ("dp", "fsdp"), axis=0, tiled=True),
            lax.all_gather(midnorm, ("dp", "fsdp"), axis=0, tiled=True),
        )
        back_qkv, back_proj, back_expand, back_contract, back_pre, back_mid = full_bwd
        back_pre = back_pre.astype(jnp.float32)
        back_mid = back_mid.astype(jnp.float32)
        grad_rows = cotangent[batch_idx].astype(jnp.float32)
        ffn_grad = (row_mask * grad_rows).astype(jnp.bfloat16)
        term_contract = jnp.einsum(
            "rf,rd->fd", hidden, ffn_grad, preferred_element_type=jnp.float32
        )
        hidden_grad = jnp.einsum(
            "rd,fd->rf", ffn_grad, back_contract, preferred_element_type=jnp.float32
        )
        expand_grad = jax.vjp(geglu, expanded)[1](hidden_grad)[0].astype(jnp.bfloat16)
        term_expand = jnp.einsum(
            "rd,re->de", normed_two, expand_grad, preferred_element_type=jnp.float32
        )
        two_grad = jnp.einsum(
            "re,de->rd", expand_grad, back_expand, preferred_element_type=jnp.float32
        )
        mid_part, term_midnorm = jax.vjp(layer_norm, mid_rows, back_mid)[1](two_grad)
        mid_grad = grad_rows + mid_part
        attn_grad = (row_mask * mid_grad).astype(jnp.bfloat16)
        term_proj = jnp.einsum("rd,re->de", attended, attn_grad, preferred_element_type=jnp.float32)
        attended_grad = jnp.einsum(
            "re,de->rd", attn_grad, back_proj, preferred_element_type=jnp.float32
        ).astype(jnp.bfloat16)
        attended_grad = attended_grad.reshape(blocks_here, block_rows, head_count, head_size)
        scores_back = (
            jnp.einsum(
                "brhe,bche->bhrc", query_tiles, key_tiles, preferred_element_type=jnp.float32
            )
            * score_scale
        )
        scores_back = jnp.where(allowed, scores_back, masked_score)
        prob_back = jnp.exp(scores_back - log_total)
        prob_back_low = prob_back.astype(jnp.bfloat16)
        prob_grad = jnp.einsum(
            "brhe,bche->bhrc", attended_grad, value_tiles, preferred_element_type=jnp.float32
        )
        value_tile_grad = jnp.einsum(
            "bhrc,brhe->bche", prob_back_low, attended_grad, preferred_element_type=jnp.float32
        )
        score_grad = prob_back * (
            prob_grad - jnp.sum(prob_back * prob_grad, axis=-1, keepdims=True)
        )
        score_grad = score_grad.astype(jnp.bfloat16)
        query_grad = (
            jnp.einsum("bhrc,bche->brhe", score_grad, key_tiles, preferred_element_type=jnp.float32)
            * score_scale
        )
        key_tile_grad = (
            jnp.einsum(
                "bhrc,brhe->bche", score_grad, query_tiles, preferred_element_type=jnp.float32
            )
            * score_scale
        )
        tile_grads = jnp.stack(
            [
                key_tile_grad.reshape(blocks_here, 2 * block_rows, model_width),
                value_tile_grad.reshape(blocks_here, 2 * block_rows, model_width),
            ]
        )
        pred_grads = tile_grads[:, :, :half_rows]
        own_grads = tile_grads[:, :, half_rows : half_rows + block_rows]
        succ_grads = tile_grads[:, :, half_rows + block_rows :]
        slot_ids = jnp.arange(blocks_here + 1)[:, None]
        pred_table = (pred_slot[None, :] == slot_ids).astype(jnp.float32)
        succ_table = (succ_slot[None, :] == slot_ids).astype(jnp.float32)
        routed_prev = jnp.einsum(
            "jb,kbrd->kjrd", pred_table, pred_grads, precision=lax.Precision.HIGHEST
        )
        routed_next = jnp.einsum(
            "jb,kbrd->kjrd", succ_table, succ_grads, precision=lax.Precision.HIGHEST
        )
        returned_prev = shifted(
            routed_prev[:, blocks_here].astype(jnp.bfloat16), "fsdp", -1
        ).astype(jnp.float32)
        returned_next = shifted(routed_next[:, blocks_here].astype(jnp.bfloat16), "fsdp", 1).astype(
            jnp.float32
        )
        last_table = (jnp.arange(blocks_here) == last_slot).astype(jnp.float32)
        first_table = (jnp.arange(blocks_here) == first_slot).astype(jnp.float32)
        tail_part = (
            routed_prev[:, :blocks_here] + last_table[None, :, None, None] * returned_prev[:, None]
        )
        head_part = (
            routed_next[:, :blocks_here] + first_table[None, :, None, None] * returned_next[:, None]
        )
        kv_grads = own_grads + jnp.concatenate([head_part, tail_part], axis=2)
        query_rows_grad = rope_back(
            query_grad.reshape(row_count, head_count, head_size), cos_table, sin_table
        )
        key_rows_grad = rope_back(
            kv_grads[0].reshape(row_count, head_count, head_size), cos_table, sin_table
        )
        qkv_delta = jnp.concatenate(
            [
                query_rows_grad.reshape(row_count, model_width),
                key_rows_grad.reshape(row_count, model_width),
                kv_grads[1].reshape(row_count, model_width),
            ],
            axis=1,
        ).astype(jnp.bfloat16)
        term_qkv = jnp.einsum(
            "rd,re->de", normed_one, qkv_delta, preferred_element_type=jnp.float32
        )
        one_grad = jnp.einsum("re,de->rd", qkv_delta, back_qkv, preferred_element_type=jnp.float32)
        input_part, term_prenorm = jax.vjp(layer_norm, x_rows, back_pre)[1](one_grad)
        input_grads.append((mid_grad + input_part).astype(jnp.bfloat16))
        new_terms = (term_qkv, term_proj, term_expand, term_contract, term_prenorm, term_midnorm)
        if grad_totals is None:
            grad_totals = tuple(new_terms)
        else:
            grad_totals = tuple(
                (running + increment for running, increment in zip(grad_totals, new_terms))
            )
    grad_shards = (
        lax.psum_scatter(grad_totals[0], ("dp", "fsdp"), scatter_dimension=0, tiled=True),
        lax.psum_scatter(grad_totals[1], ("dp", "fsdp"), scatter_dimension=0, tiled=True),
        lax.psum_scatter(grad_totals[2], ("dp", "fsdp"), scatter_dimension=0, tiled=True),
        lax.psum_scatter(grad_totals[3], ("dp", "fsdp"), scatter_dimension=1, tiled=True),
        lax.psum_scatter(grad_totals[4], ("dp", "fsdp"), scatter_dimension=0, tiled=True),
        lax.psum_scatter(grad_totals[5], ("dp", "fsdp"), scatter_dimension=0, tiled=True),
    )
    return (
        jnp.stack(results),
        jnp.stack(input_grads),
        grad_shards[0],
        grad_shards[1],
        grad_shards[2],
        grad_shards[3],
        grad_shards[4],
        grad_shards[5],
    )


def solution(mesh):
    return jax.shard_map(
        local,
        mesh=mesh,
        in_specs=(
            P(None, ("dp", "fsdp"), None),
            P(None, ("dp", "fsdp"), None),
            P(("dp", "fsdp"), None),
            P(("dp", "fsdp"), None),
            P(("dp", "fsdp"), None),
            P(None, ("dp", "fsdp")),
            P(("dp", "fsdp")),
            P(("dp", "fsdp")),
            P(None, "dp", None),
            P(None, ("dp", "fsdp")),
            P(None, None, ("dp", "fsdp")),
            P(None, ("dp", "fsdp")),
        ),
        out_specs=(
            P(None, ("dp", "fsdp"), None),
            P(None, ("dp", "fsdp"), None),
            P(("dp", "fsdp"), None),
            P(("dp", "fsdp"), None),
            P(("dp", "fsdp"), None),
            P(None, ("dp", "fsdp")),
            P(("dp", "fsdp")),
            P(("dp", "fsdp")),
        ),
        check_vma=False,
    )
```

profile of v0, /device:TPU:0, one launch (start us, length us, event | category | flops | bytes accessed | tf_op | source)
XLA Modules:
  0.0 816.4 jit_solution(13785037167878608489)
XLA Ops:
  27.0 44.7 %all-reduce.10 = (bf16[768]{0:T(1024)(128)(2,1)S(1)}, bf16[768]{0:T(1024)(128)(2,1)S(1)}) all-reduce(bf16[768]{0:T(1024)(128)(2,1)S(1)} %dynamic-update-slice, bf16[768]{0:T(1024)(128)(2,1)S(1)} %dynamic-update-slice.1), channel_id=1, replica_groups=mesh['dp'=4,'fsdp'=8] {'dp','fsdp'}, use_global_device_ids=true, to_apply=%add.4 | all-reduce | flops 1536 | bytes 6144
  95.4 5.8 copy.171
  101.2 5.1 fusion.101
  106.3 3.6 fusion.227
  117.8 5.1 fusion.98
  122.9 3.6 fusion.228
  133.4 3.7 convert_element_type.343
  137.2 3.5 convert_element_type.344
  144.7 3.4 mul.746
  194.9 5.5 collective-permute-start.3
  204.8 3.8 squeeze.103
  208.7 6.5 fusion.73
  258.4 4.8 fusion.233
  267.2 4.8 fusion.89
  277.5 4.9 fusion.235
  286.5 4.8 fusion.88
  298.6 7.8 fusion.222
  306.4 9.3 %fusion.128 = (f32[640,1152]{1,0:T(8,128)S(1)}, f32[640,1152]{1,0:T(8,128)S(1)}, f32[640,1152]{1,0:T(8,128)S(1)}) fusion(f32[640,2304]{1,0:T(8,128)} %fusion.222, bf16[1152,768]{0,1:T(8,128)(2,1)} %all-gather.11.cloned.1.call-done, f32[640]{0:T(1024)S(1)} %get-tuple-element.178, bf16[2,640,768]{2,1,0:T(8,128)(2,1)S(1)} %copy-done.31), kind=kOutput, calls=%fused_computation.290 | convolution fusion | flops 1181859840 | bytes 14553088 | tf_op jit(solution)/shard_map/rd,fd->rf/dot_general | solution.py:220
  322.2 7.1 fusion.129
  334.8 3.7 multiply_reduce_fusion.3
  350.8 3.5 convolution_convert_fusion.1
  354.4 4.3 reshape.1125
  358.7 4.3 copy.207
  363.8 3.6 fusion.152
  367.5 3.7 convolution_add_fusion.2
  371.2 8.8 %multiply_reduce_fusion.1 = (f32[5,12,128]{2,1,0:T(8,128)S(1)}, f32[5,12,128,256]{3,2,1,0:T(8,128)}) fusion(f32[5,12,128,256]{3,2,1,0:T(8,128)} %copy-done.1, f32[5,12,128]{2,1,0:T(8,128)S(1)} %log_add_fusion.1, bf16[5,128,12,64]{1,3,2,0:T(8,128)(2,1)} %copy.207, bf16[5,64,12,64]{1,3,2,0:T(8,128)(2,1)} %bitcast.508, bf16[5,128,12,64]{1,3,2,0:T(8,128)(2,1)} %copy.180, ...), kind=kOutput, calls=%fused_computation.18 | convolution fusion | flops 263447040 | bytes 18739200 | tf_op jit(solution)/shard_map/brhe,bche->bhrc/dot_general | solution.py:247
  380.0 7.2 multiply_convert_fusion.1
  390.5 6.3 copy.211
  396.7 5.8 fusion.10
  402.5 6.2 copy.212
  408.8 3.8 fusion.79
  430.2 3.8 copy.219
  434.1 6.6 fusion.134
  440.7 5.7 convolution_add_fusion
  447.9 6.8 multiply_reduce_fusion
  454.8 5.2 multiply_convert_fusion
  463.2 6.3 copy.223
  469.5 5.7 fusion.8
  475.2 6.3 copy.224
  481.5 3.9 fusion.81
  488.2 5.1 collective-permute-start.8
  516.4 4.0 slice.557
  569.4 6.1 convolution_add_fusion.1
  576.2 4.3 fusion.90
  592.5 45.3 %all-reduce.9 = (f32[768]{0:T(1024)S(1)}, f32[768]{0:T(1024)S(1)}) all-reduce(f32[768]{0:T(1024)S(1)} %add.329, f32[768]{0:T(1024)S(1)} %add.330), channel_id=6, replica_groups=mesh['dp'=4,'fsdp'=8] {'dp','fsdp'}, use_global_device_ids=true, to_apply=%region_38.42.clone | all-reduce | flops 1536 | bytes 12288
  639.0 4.9 fusion.95
  645.3 39.1 %reduce-scatter.11.cloned.1.call-done = f32[24,2304]{1,0:T(8,128)} async-done(((f32[768,2304]{1,0:T(8,128)}), f32[24,2304]{1,0:T(8,128)}) %reduce-scatter.11.cloned.1.call-update) | async-done | bytes 221200 | tf_op jit(solution)/shard_map/reduce_scatter | solution.py:330
  684.4 124.9 %reduce-scatter.7.cloned.1.call-done = f32[24,2304]{1,0:T(8,128)} async-done(((f32[768,2304]{1,0:T(8,128)}), f32[24,2304]{1,0:T(8,128)}) %reduce-scatter.7.cloned.1.call-update) | async-done | bytes 221200 | tf_op jit(solution)/shard_map/reduce_scatter | solution.py:328
  (641 shorter events, 309.0 us)
Async XLA Ops:
  7.2 18.1 %copy-start.8 = (bf16[2,640,768]{2,1,0:T(8,128)(2,1)S(1)}, bf16[2,640,768]{2,1,0:T(8,128)(2,1)}, u32[]{:S(2)}) copy-start(bf16[2,640,768]{2,1,0:T(8,128)(2,1)} %param.18) | copy-start | bytes 5898244
  7.2 88.2 %all-gather.5.cloned.1.call-start = ((), (), s32[]{:S(2)}) async-start(), calls=%async_computation.4 | async-start | bytes 3649536 | tf_op jit(solution)/shard_map/all_gather | solution.py:104
  7.9 285.3 %all-gather.7.cloned.1.call-start = ((), (), s32[]{:S(2)}) async-start(), calls=%async_computation.5 | async-start | bytes 1216512 | tf_op jit(solution)/shard_map/all_gather | solution.py:105
  8.7 290.0 %all-gather.9.cloned.1.call-start = ((), (), s32[]{:S(2)}) async-start(), calls=%async_computation.6 | async-start | bytes 3649536 | tf_op jit(solution)/shard_map/all_gather | solution.py:106
  9.4 17.1 %copy-start.164 = (bf16[24]{0:T(256)(128)(2,1)S(1)}, bf16[24]{0:T(256)(128)(2,1)}, u32[]{:S(2)}) copy-start(bf16[24]{0:T(256)(128)(2,1)} %param.24) | copy-start | bytes 148
  9.4 17.3 %copy-start.165 = (bf16[24]{0:T(256)(128)(2,1)S(1)}, bf16[24]{0:T(256)(128)(2,1)}, u32[]{:S(2)}) copy-start(bf16[24]{0:T(256)(128)(2,1)} %param.25) | copy-start | bytes 148
  9.4 297.0 %all-gather.11.cloned.1.call-start = ((), (), s32[]{:S(2)}) async-start(), calls=%async_computation.7 | async-start | bytes 1824768 | tf_op jit(solution)/shard_map/all_gather | solution.py:107
  14.4 353.0 %copy-start.137 = (f32[640]{0:T(1024)}, f32[640]{0:T(1024)S(1)}, u32[]{:S(2)}) copy-start(f32[640]{0:T(1024)S(1)} %get-tuple-element.178) | copy-start | bytes 7684
  14.5 78.6 %collective-permute-start.5 = (bf16[64]{0:T(256)(128)(2,1)S(1)}, bf16[64]{0:T(256)(128)(2,1)S(1)}, u32[]{:S(2)}, u32[]{:S(2)}) collective-permute-start(bf16[64]{0:T(256)(128)(2,1)S(1)} %slice_bitcast_fusion.2), channel_id=1, source_target_pairs={{1,0},{2,1},{3,2},{4,3},{5,4},{6,5},{7,6},{9,8},{10,9},{11,10},{12... | collective-permute-start | bytes 392 | tf_op jit(solution)/shard_map/ppermute | solution.py:17
  18.7 75.0 %collective-permute-start.2 = (bf16[64]{0:T(256)(128)(2,1)S(1)}, bf16[64]{0:T(256)(128)(2,1)S(1)}, u32[]{:S(2)}, u32[]{:S(2)}) collective-permute-start(bf16[64]{0:T(256)(128)(2,1)S(1)} %slice_bitcast_fusion.6), channel_id=1, source_target_pairs={{1,0},{2,1},{3,2},{4,3},{5,4},{6,5},{7,6},{9,8},{10,9},{11,10},{12... | collective-permute-start | bytes 392 | tf_op jit(solution)/shard_map/ppermute | solution.py:17
  20.1 625.2 %reduce-scatter.9.cloned.1.call-start = ((), (), s32[]{:S(2)}) async-start(), calls=%async_computation.9 | async-start | bytes 2433024 | tf_op jit(solution)/shard_map/reduce_scatter | solution.py:329
  25.3 47.8 %copy-start.95 = (f32[640,64]{0,1:T(8,128)}, f32[640,64]{0,1:T(8,128)S(1)}, u32[]{:S(2)}) copy-start(f32[640,64]{0,1:T(8,128)S(1)} %get-tuple-element.121) | copy-start | bytes 491524
  25.3 117.0 %copy-start.97 = (f32[640,64]{0,1:T(8,128)}, f32[640,64]{0,1:T(8,128)S(1)}, u32[]{:S(2)}) copy-start(f32[640,64]{0,1:T(8,128)S(1)} %get-tuple-element.122) | copy-start | bytes 491524
  25.7 75.5 %copy-start.125 = (f32[640]{0:T(1024)}, f32[640]{0:T(1024)S(1)}, u32[]{:S(2)}) copy-start(f32[640]{0:T(1024)S(1)} %get-tuple-element.196) | copy-start | bytes 7684
  25.7 92.1 %copy-start.114 = (f32[640]{0:T(1024)}, f32[640]{0:T(1024)S(1)}, u32[]{:S(2)}) copy-start(f32[640]{0:T(1024)S(1)} %get-tuple-element.195) | copy-start | bytes 7684
  26.4 50.1 %copy-start.133 = (f32[640]{0:T(1024)}, f32[640]{0:T(1024)S(1)}, u32[]{:S(2)}) copy-start(f32[640]{0:T(1024)S(1)} %get-tuple-element.23) | copy-start | bytes 7684
  26.4 55.7 %copy-start.135 = (f32[640]{0:T(1024)}, f32[640]{0:T(1024)S(1)}, u32[]{:S(2)}) copy-start(f32[640]{0:T(1024)S(1)} %get-tuple-element.24) | copy-start | bytes 7684
  26.4 74.7 %copy-start.127 = (f32[640]{0:T(1024)}, f32[640]{0:T(1024)S(1)}, u32[]{:S(2)}) copy-start(f32[640]{0:T(1024)S(1)} %fusion.181) | copy-start | bytes 7684
  71.7 46.1 %copy-start.112 = (f32[768]{0:T(1024)}, f32[768]{0:T(1024)S(1)}, u32[]{:S(2)}) copy-start(f32[768]{0:T(1024)S(1)} %convert_element_type.336) | copy-start | bytes 9220
  80.2 14.0 %copy-start.147 = (pred[5]{0:T(512)(128)(4,1)}, pred[5]{0:T(512)(128)(4,1)S(1)}, u32[]{:S(2)}) copy-start(pred[5]{0:T(512)(128)(4,1)S(1)} %get-tuple-element.143) | copy-start | bytes 19
  82.1 92.1 %copy-start.100 = (f32[640,64]{0,1:T(8,128)}, f32[640,64]{0,1:T(8,128)S(1)}, u32[]{:S(2)}) copy-start(f32[640,64]{0,1:T(8,128)S(1)} %get-tuple-element.126) | copy-start | bytes 491524
  82.2 35.6 %copy-start.123 = (f32[640]{0:T(1024)}, f32[640]{0:T(1024)S(1)}, u32[]{:S(2)}) copy-start(f32[640]{0:T(1024)S(1)} %fusion.183) | copy-start | bytes 7684
  162.5 65.0 %collective-permute-start = (bf16[2,64,768]{2,1,0:T(8,128)(2,1)}, bf16[2,64,768]{2,1,0:T(8,128)(2,1)}, u32[]{:S(2)}, u32[]{:S(2)}) collective-permute-start(bf16[2,64,768]{2,1,0:T(8,128)(2,1)} %slice.348), channel_id=1, source_target_pairs={{0,1},{1,2},{2,3},{3,4},{4,5},{5,6},{6,7},{8,9},{9,10},{10,11},{11... | collective-permute-start | bytes 589832 | tf_op jit(solution)/shard_map/ppermute | solution.py:17
  165.5 68.2 %collective-permute-start.1 = (bf16[2,64,768]{2,1,0:T(8,128)(2,1)}, bf16[2,64,768]{2,1,0:T(8,128)(2,1)}, u32[]{:S(2)}, u32[]{:S(2)}) collective-permute-start(bf16[2,64,768]{2,1,0:T(8,128)(2,1)} %slice.352), channel_id=1, source_target_pairs={{1,0},{2,1},{3,2},{4,3},{5,4},{6,5},{7,6},{9,8},{10,9},{11,10},{12... | collective-permute-start | bytes 589832 | tf_op jit(solution)/shard_map/ppermute | solution.py:17
  194.9 45.3 %collective-permute-start.3 = (bf16[2,64,768]{2,1,0:T(8,128)(2,1)}, bf16[2,64,768]{2,1,0:T(8,128)(2,1)}, u32[]{:S(2)}, u32[]{:S(2)}) collective-permute-start(bf16[2,64,768]{2,1,0:T(8,128)(2,1)} %slice.367), channel_id=1, source_target_pairs={{0,1},{1,2},{2,3},{3,4},{4,5},{5,6},{6,7},{8,9},{9,10},{10,11},{11... | collective-permute-start | bytes 589832 | tf_op jit(solution)/shard_map/ppermute | solution.py:17
  201.2 45.7 %collective-permute-start.4 = (bf16[2,64,768]{2,1,0:T(8,128)(2,1)}, bf16[2,64,768]{2,1,0:T(8,128)(2,1)}, u32[]{:S(2)}, u32[]{:S(2)}) collective-permute-start(bf16[2,64,768]{2,1,0:T(8,128)(2,1)} %slice.371), channel_id=1, source_target_pairs={{1,0},{2,1},{3,2},{4,3},{5,4},{6,5},{7,6},{9,8},{10,9},{11,10},{12... | collective-permute-start | bytes 589832 | tf_op jit(solution)/shard_map/ppermute | solution.py:17
  298.6 40.0 %copy-start.143 = (f32[640]{0:T(1024)}, f32[640]{0:T(1024)S(1)}, u32[]{:S(2)}) copy-start(f32[640]{0:T(1024)S(1)} %fusion.182) | copy-start | bytes 7684
  306.4 9.3 %copy-start.57 = (f32[640,2304]{1,0:T(8,128)S(1)}, f32[640,2304]{1,0:T(8,128)}, u32[]{:S(2)}) copy-start(f32[640,2304]{1,0:T(8,128)} %fusion.222) | copy-start | bytes 17694724
  315.7 16.5 %copy-start.88 = (f32[640,1152]{1,0:T(8,128)}, f32[640,1152]{1,0:T(8,128)S(1)}, u32[]{:S(2)}) copy-start(f32[640,1152]{1,0:T(8,128)S(1)} %get-tuple-element.41) | copy-start | bytes 8847364
  319.4 12.8 %copy-start.34 = (f32[640,1152]{1,0:T(8,128)}, f32[640,1152]{1,0:T(8,128)S(1)}, u32[]{:S(2)}) copy-start(f32[640,1152]{1,0:T(8,128)S(1)} %get-tuple-element.55) | copy-start | bytes 8847364
  319.4 48.1 %copy-start.36 = (bf16[640,1152]{1,0:T(8,128)(2,1)}, bf16[640,1152]{1,0:T(8,128)(2,1)S(1)}, u32[]{:S(2)}) copy-start(bf16[640,1152]{1,0:T(8,128)(2,1)S(1)} %get-tuple-element.56) | copy-start | bytes 4423684
  346.6 298.7 %reduce-scatter.13.cloned.1.call-start = ((), (), s32[]{:S(2)}) async-start(), calls=%async_computation.11 | async-start | bytes 3649536
  354.4 9.4 %copy-start.141 = (f32[640]{0:T(1024)S(1)}, f32[640]{0:T(1024)}, u32[]{:S(2)}) copy-start(f32[640]{0:T(1024)} %get-tuple-element.174) | copy-start | bytes 7684
  380.0 304.4 %reduce-scatter.11.cloned.1.call-start = ((), (), s32[]{:S(2)}) async-start(), calls=%async_computation.10 | async-start | bytes 7299072 | tf_op jit(solution)/shard_map/reduce_scatter | solution.py:330
  413.1 90.5 %collective-permute-start.6 = (bf16[2,64,768]{2,1,0:T(8,128)(2,1)S(1)}, bf16[2,64,768]{2,1,0:T(8,128)(2,1)S(1)}, u32[]{:S(2)}, u32[]{:S(2)}) collective-permute-start(bf16[2,64,768]{2,1,0:T(8,128)(2,1)S(1)} %bitcast.529), channel_id=1, source_target_pairs={{0,1},{1,2},{2,3},{3,4},{4,5},{5,6},{6,7},{8,9},{9,10},{10,11},{11... | collective-permute-start | bytes 589832 | tf_op jit(solution)/shard_map/ppermute | solution.py:17
  419.5 84.1 %collective-permute-start.7 = (bf16[2,64,768]{2,1,0:T(8,128)(2,1)}, bf16[2,64,768]{2,1,0:T(8,128)(2,1)}, u32[]{:S(2)}, u32[]{:S(2)}) collective-permute-start(bf16[2,64,768]{2,1,0:T(8,128)(2,1)} %bitcast.476), channel_id=1, source_target_pairs={{1,0},{2,1},{3,2},{4,3},{5,4},{6,5},{7,6},{9,8},{10,9},{11,10},{12... | collective-permute-start | bytes 589832 | tf_op jit(solution)/shard_map/ppermute | solution.py:17
  446.5 362.8 %reduce-scatter.7.cloned.1.call-start = ((), (), s32[]{:S(2)}) async-start(), calls=%async_computation.8 | async-start | bytes 7299072 | tf_op jit(solution)/shard_map/reduce_scatter | solution.py:328
  481.5 11.8 %copy-start.7 = (bf16[5,12,128,256]{3,2,1,0:T(8,128)(2,1)S(1)}, bf16[5,12,128,256]{3,2,1,0:T(8,128)(2,1)}, u32[]{:S(2)}) copy-start(bf16[5,12,128,256]{3,2,1,0:T(8,128)(2,1)} %copy-done.6) | copy-start | bytes 11796484
  481.5 11.8 %copy-start.77 = (bf16[5,128,12,64]{1,3,2,0:T(8,128)(2,1)S(1)}, bf16[5,128,12,64]{1,3,2,0:T(8,128)(2,1)}, u32[]{:S(2)}) copy-start(bf16[5,128,12,64]{1,3,2,0:T(8,128)(2,1)} %get-tuple-element.111) | copy-start | bytes 2949124
  481.5 11.8 %copy-start.79 = (bf16[1,5,64,768]{2,3,1,0:T(8,128)(2,1)S(1)}, bf16[1,5,64,768]{2,3,1,0:T(8,128)(2,1)}, u32[]{:S(2)}) copy-start(bf16[1,5,64,768]{2,3,1,0:T(8,128)(2,1)} %copy.201) | copy-start | bytes 1474564
  481.5 11.8 %copy-start.80 = (bf16[1,5,64,768]{2,3,1,0:T(8,128)(2,1)S(1)}, bf16[1,5,64,768]{2,3,1,0:T(8,128)(2,1)}, u32[]{:S(2)}) copy-start(bf16[1,5,64,768]{2,3,1,0:T(8,128)(2,1)} %copy.204) | copy-start | bytes 1474564
  481.5 14.3 %copy-start.3 = (f32[1,5,256,768]{3,1,2,0:T(8,128)S(1)}, f32[1,5,256,768]{3,1,2,0:T(8,128)}, u32[]{:S(2)}) copy-start(f32[1,5,256,768]{3,1,2,0:T(8,128)} %copy.224) | copy-start | bytes 11796484
  488.2 32.2 %collective-permute-start.8 = (bf16[2,64,768]{2,1,0:T(8,128)(2,1)}, bf16[2,64,768]{2,1,0:T(8,128)(2,1)}, u32[]{:S(2)}, u32[]{:S(2)}) collective-permute-start(bf16[2,64,768]{2,1,0:T(8,128)(2,1)} %bitcast.475), channel_id=1, source_target_pairs={{0,1},{1,2},{2,3},{3,4},{4,5},{5,6},{6,7},{8,9},{9,10},{10,11},{11... | collective-permute-start | bytes 589832 | tf_op jit(solution)/shard_map/ppermute | solution.py:17
  495.8 9.5 %copy-start.158 = (f32[5]{0:T(128)S(1)}, f32[5]{0:T(128)}, u32[]{:S(2)}) copy-start(f32[5]{0:T(128)} %get-tuple-element.206) | copy-start | bytes 64
  495.9 10.0 %copy-start.20 = (f32[2,6,64,768]{3,1,2,0:T(8,128)S(1)}, f32[2,6,64,768]{3,1,2,0:T(8,128)}, u32[]{:S(2)}) copy-start(f32[2,6,64,768]{3,1,2,0:T(8,128)} %copy-done.19) | copy-start | bytes 7077892
  499.2 22.9 %collective-permute-start.9 = (bf16[2,64,768]{2,1,0:T(8,128)(2,1)}, bf16[2,64,768]{2,1,0:T(8,128)(2,1)}, u32[]{:S(2)}, u32[]{:S(2)}) collective-permute-start(bf16[2,64,768]{2,1,0:T(8,128)(2,1)} %bitcast.474), channel_id=1, source_target_pairs={{1,0},{2,1},{3,2},{4,3},{5,4},{6,5},{7,6},{9,8},{10,9},{11,10},{12... | collective-permute-start | bytes 589832 | tf_op jit(solution)/shard_map/ppermute | solution.py:17
  590.6 48.4 %copy-start.130 = (f32[640]{0:T(1024)S(1)}, f32[640]{0:T(1024)}, u32[]{:S(2)}) copy-start(f32[640]{0:T(1024)} %copy-done.129) | copy-start | bytes 7684
  590.6 48.4 %copy-start.132 = (f32[640]{0:T(1024)S(1)}, f32[640]{0:T(1024)}, u32[]{:S(2)}) copy-start(f32[640]{0:T(1024)} %copy-done.131) | copy-start | bytes 7684
  (149 other events, 624.7 us)
Sparse Core Ops, SparseCore 0:
  10.9 62.8 all-gather.4
  76.7 52.7 all-gather.6
  132.4 58.8 all-gather.8
  194.0 54.2 all-gather.10
  346.8 102.3 reduce-scatter.8
  455.0 104.5 reduce-scatter.12
  565.8 118.5 reduce-scatter.10
  690.7 118.5 reduce-scatter.6
where the time goes:
time: 823 us; the launch traced here: 816 us
  local copies, waits for them, and re-layouts  247 us (30%)
  waiting for transfers between devices  166 us (20%)
  matrix products  165 us (20%)
  other arithmetic  100 us (12%)
  blocking collectives  90 us (11%)
  starting transfers between devices  24.5 us (3%)
  between operations  24.3 us (3%)
    reduce_scatter x1, waiting for transfers between devices, local(): lax.psum_scatter(grad_totals[0], ('dp', 'fsdp'), scatter_dimension=0, til...  125 us
    unnamed x2, blocking collectives  90 us
    reduce_scatter x1, waiting for transfers between devices, local(): lax.psum_scatter(grad_totals[2], ('dp', 'fsdp'), scatter_dimension=0, til...  39.1 us
    unnamed x368, local copies, waits for them, and re-layouts  33.9 us
    mul x10, local copies, waits for them, and re-layouts, apply_rope(): return values * cos_table + rotate_half(values) * sin_table  29.3 us
    another operation x4, local copies, waits for them, and re-layouts, local(): jnp.stack([key_tile_grad.reshape(blocks_here, 2 * block_rows, model_width...  25 us
    ppermute x10, starting transfers between devices, shifted(): return lax.ppermute(block, axis, route)  24.2 us
    convert_element_type x8, local copies, waits for them, and re-layouts, local(): value_own = qkv_full[:, 2].astype(jnp.bfloat16)  22 us
  transfers between devices with their start and end apart: 18, of which 2 were waited for; matrix products, arithmetic and copies ran while one was open for 55% of the time, Pallas kernels for 0%

commit v1 on v0

v1 whole, which is shorter than its diff:
```python
import functools

import jax
import jax.numpy as jnp
import numpy as np
from jax import lax
from jax.experimental import pallas as pl
from jax.experimental.pallas import tpu as pltpu
from jax.sharding import PartitionSpec as P

HEAD_DIM = 64
PAIR = 128
STEP_SLOTS = 2
CHUNK = 32
norm_epsilon = 1e-05
rope_base = 10000.0
masked_score = -1e30
F32 = jnp.float32
BF16 = jnp.bfloat16
VMEM_LIMIT = 60 * 1024 * 1024


def nn(a, b):
    return lax.dot_general(a, b, (((1,), (0,)), ((), ())), preferred_element_type=F32)


def nt(a, b):
    return lax.dot_general(a, b, (((1,), (1,)), ((), ())), preferred_element_type=F32)


def tn(a, b):
    return lax.dot_general(a, b, (((0,), (0,)), ((), ())), preferred_element_type=F32)


def rope_tables(most_offset, block_rows):
    half = HEAD_DIM // 2
    freq = rope_base ** (-np.arange(half) * (2.0 / HEAD_DIM))
    freq = np.tile(freq, PAIR // half)
    sign = np.where(np.arange(PAIR) % HEAD_DIM < half, -1.0, 1.0)

    def pair(positions):
        angles = positions[:, None] * freq[None, :]
        return (
            jnp.asarray(np.cos(angles), F32),
            jnp.asarray(np.sin(angles) * sign[None, :], F32),
        )

    return (*pair(np.arange(most_offset) * float(block_rows)), *pair(np.arange(block_rows) * 1.0))


def slot_scalars(lengths, dealing, slot, blocks, group):
    micro = slot // blocks
    place = slot - micro * blocks
    block = dealing[micro, place]
    within = lax.rem(block, group)
    begin = jnp.int32(0)
    start = jnp.int32(0)
    ends = jnp.int32(0)
    for seq in range(lengths.shape[1]):
        begin = jnp.where(start <= within, start, begin)
        start = start + lengths[micro, seq]
        ends = ends + jnp.where(start - 1 == within, 1, 0)
    return micro, place, lax.rem(block, blocks), within - begin, ends > 0


def slot_angles(offset, ca, sa, cb, sb):
    first_c, first_s = ca[pl.ds(offset, 1), :], sa[pl.ds(offset, 1), :]
    return first_c * cb[...] - first_s * sb[...], first_s * cb[...] + first_c * sb[...]


def swap_halves(v):
    low = lax.broadcasted_iota(jnp.int32, v.shape, 1) % HEAD_DIM < HEAD_DIM // 2
    return jnp.where(low, pltpu.roll(v, PAIR - HEAD_DIM // 2, 1), pltpu.roll(v, HEAD_DIM // 2, 1))


def head_masks(dtype):
    low = lax.broadcasted_iota(jnp.int32, (1, PAIR), 1) < HEAD_DIM
    return low.astype(F32).astype(dtype), (1.0 - low.astype(F32)).astype(dtype)


def two_heads(tile):
    even, odd = head_masks(tile.dtype)
    return jnp.concatenate([tile * even, tile * odd], axis=0)


def from_heads(t, rows):
    return jnp.concatenate([t[:HEAD_DIM, :rows], t[HEAD_DIM:, rows:]], axis=0).T


def chunk_rows(c, size=CHUNK):
    return pl.ds(pl.multiple_of(c * size, size), size)


def qkv_kernel(
    blocks, group, rows, width,
    lengths, dealing, counts, x, w_all, gain, ca, sa, cb, sb,
    q, k, v, normed, to_next, to_prev,
    w, full, cos, sin, sem,
):
    step = pl.program_id(0)
    half = rows // 2

    @pl.when(step == 0)
    def _():
        copy = pltpu.make_async_copy(w_all.at[:, pl.ds(0, 3 * width)], w, sem)
        copy.start()
        copy.wait()

    slots = [slot_scalars(lengths, dealing, step * STEP_SLOTS + t, blocks, group) for t in range(STEP_SLOTS)]
    for t, (_, _, _, offset, _) in enumerate(slots):
        c, s = slot_angles(offset, ca, sa, cb, sb)
        cos[t * rows : (t + 1) * rows, :] = c
        sin[t * rows : (t + 1) * rows, :] = s

    def norm(c, carry):
        at = chunk_rows(c)
        xf = x[at, :].astype(F32)
        centred = xf - jnp.mean(xf, axis=-1, keepdims=True)
        spread = jnp.mean(centred * centred, axis=-1, keepdims=True)
        normed[at, :] = (centred * lax.rsqrt(spread + norm_epsilon) * gain[...]).astype(BF16)
        return carry

    lax.fori_loop(0, STEP_SLOTS * rows // CHUNK, norm, 0)
    for n in range(0, 3 * width, 256):
        full[:, n : n + 256] = nn(normed[...], w[:, n : n + 256])

    def turn(c, carry):
        at = chunk_rows(c)
        co, si = cos[at, :], sin[at, :]
        for p in range(width // PAIR):
            lanes = slice(p * PAIR, (p + 1) * PAIR)
            for out, base in ((q, 0), (k, width)):
                tile = full[at, base + p * PAIR : base + (p + 1) * PAIR]
                out[at, lanes] = (tile * co + swap_halves(tile) * si).astype(BF16)
            v[at, lanes] = full[at, 2 * width + p * PAIR : 2 * width + (p + 1) * PAIR].astype(BF16)
        return carry

    lax.fori_loop(0, STEP_SLOTS * rows // CHUNK, turn, 0)
    for t, (micro, _, local, _, _) in enumerate(slots):
        base = t * rows

        @pl.when(local == blocks - 1)
        def _(micro=micro, base=base):
            to_next[micro, :half, :] = k[base + half : base + rows, :]
            to_next[micro, half:, :] = v[base + half : base + rows, :]

        @pl.when(local == 0)
        def _(micro=micro, base=base):
            to_prev[micro, :half, :] = k[base : base + half, :]
            to_prev[micro, half:rows, :] = v[base : base + half, :]
            valid = jnp.full((16, width), counts[micro, 0], jnp.int32).astype(F32)
            to_prev[micro, rows:, :] = valid.astype(BF16)


def layer_kernel(
    blocks, group, rows, width, hidden_units,
    lengths, dealing, holders, counts,
    q, k, v, from_prev, from_next, x, cot, w_all, gain, ca, sa, cb, sb,
    result, mid_grad, dq, hid, ffn_grad, normed, exp_grad, attended, attn_grad,
    dk, dv, back_prev, back_next, mid_term,
    wp, we, wc, kt, vt, bias, probs, expanded, wide, mid, hat, root, att_grad, tiles, sem,
):
    step = pl.program_id(0)
    half = rows // 2
    total = STEP_SLOTS * rows
    pairs = width // PAIR

    def weights():
        at = 3 * width
        out = []
        for place, (dst, cols) in enumerate(((we, 2 * hidden_units), (wc, hidden_units), (wp, width))):
            out.append(pltpu.make_async_copy(w_all.at[:, pl.ds(at, cols)], dst, sem.at[place]))
            at += cols
        return out

    @pl.when(step == 0)
    def _():
        for copy in weights():
            copy.start()
        dk[...] = jnp.zeros_like(dk)
        dv[...] = jnp.zeros_like(dv)
        mid_term[...] = jnp.zeros_like(mid_term)

    slots = []
    for t in range(STEP_SLOTS):
        slot = step * STEP_SLOTS + t
        micro, place, local, offset, is_last = slot_scalars(lengths, dealing, slot, blocks, group)
        pred, succ = holders[micro * 2, place], holders[micro * 2 + 1, place]
        count = counts[micro, local]
        slots.append((slot, micro, pred, succ, offset, count))
        for src, dst, part in ((k, kt, 0), (v, vt, half)):
            @pl.when(pred < blocks)
            def _(src=src, dst=dst, t=t, micro=micro, pred=pred):
                dst[t, :half, :] = src[micro * blocks + pred, half:, :]

            @pl.when(pred >= blocks)
            def _(dst=dst, part=part, t=t, micro=micro):
                dst[t, :half, :] = from_prev[micro, part : part + half, :]

            dst[t, half : half + rows, :] = src[slot]

            @pl.when(succ < blocks)
            def _(src=src, dst=dst, t=t, micro=micro, succ=succ):
                dst[t, half + rows :, :] = src[micro * blocks + succ, :half, :]

            @pl.when(succ >= blocks)
            def _(dst=dst, part=part, t=t, micro=micro):
                dst[t, half + rows :, :] = from_next[micro, part : part + half, :]

        col = lax.broadcasted_iota(jnp.int32, (2 * rows, rows), 0)
        row = lax.broadcasted_iota(jnp.int32, (2 * rows, rows), 1)
        follow = counts[micro, lax.rem(local + 1, blocks)]
        remote = from_next[micro, rows : rows + 1, :rows].astype(F32)
        follow = jnp.where(succ < blocks, jnp.full((1, rows), follow, jnp.int32).astype(F32), remote)
        follow = half + rows + jnp.minimum(follow, half)
        ends = jnp.full((1, rows), half + count, jnp.int32).astype(F32)
        high = jnp.where(is_last, ends, follow)
        lowest = jnp.where(offset > 0, 0, half)
        allowed = (col >= row) & (col - row <= rows) & (col >= lowest) & (col.astype(F32) < high)
        bias[t] = jnp.where(allowed, 0.0, masked_score)

    def attend(p, carry):
        lanes = pl.ds(pl.multiple_of(p * PAIR, PAIR), PAIR)
        for t in range(STEP_SLOTS):
            at = slice(t * rows, (t + 1) * rows)
            queries = two_heads(q[at, lanes] * jnp.asarray(HEAD_DIM**-0.5, BF16))
            scores = nt(kt[t, :, lanes], queries)
            scores = scores + jnp.concatenate([bias[t], bias[t]], axis=1)
            lifted = jnp.exp(scores - jnp.max(scores, axis=0, keepdims=True))
            prob = lifted * (1.0 / jnp.sum(lifted, axis=0, keepdims=True))
            probs[t, p] = prob
            mixed = tn(vt[t, :, lanes], prob.astype(BF16))
            attended[at, lanes] = from_heads(mixed, rows).astype(BF16)
        return carry

    lax.fori_loop(0, pairs, attend, 0)

    @pl.when(step == 0)
    def _():
        for copy in weights():
            copy.wait()

    def valid(c):
        per = rows // CHUNK
        inside = lax.rem(c, per) * CHUNK
        count = jnp.where(c < per, slots[0][5], slots[1][5])
        r = lax.broadcasted_iota(jnp.int32, (CHUNK, width), 0) + inside
        return r < count

    for n in range(0, width, 256):
        wide[:, n : n + 256] = nn(attended[...], wp[:, n : n + 256])

    def mid_norm(c, carry):
        at = chunk_rows(c)
        m = x[at, :].astype(F32) + jnp.where(valid(c), wide[at, :], 0.0)
        mid[at, :] = m
        centred = m - jnp.mean(m, axis=-1, keepdims=True)
        spread = jnp.mean(centred * centred, axis=-1, keepdims=True)
        scale = lax.rsqrt(spread + norm_epsilon)
        h = centred * scale
        hat[at, :] = h
        root[at, :] = jnp.broadcast_to(scale, (CHUNK, PAIR))
        normed[at, :] = (h * gain[...]).astype(BF16)
        ffn_grad[at, :] = jnp.where(valid(c), cot[at, :].astype(F32), 0.0).astype(BF16)
        return carry

    lax.fori_loop(0, total // CHUNK, mid_norm, 0)
    for n in range(0, 2 * hidden_units, 256):
        expanded[:, n : n + 256] = nn(normed[...], we[:, n : n + 256])

    def gate(c, carry):
        at = chunk_rows(c)
        for n in range(0, hidden_units, PAIR):
            a = expanded[at, n : n + PAIR]
            b = expanded[at, hidden_units + n : hidden_units + n + PAIR]
            phi = 0.5 + 0.5 * lax.erf(a * np.float32(0.5**0.5))
            density = np.float32((2 * np.pi) ** -0.5) * jnp.exp(a * a * -0.5)
            gelu = a * phi
            hid[at, n : n + PAIR] = (gelu * b).astype(BF16)
            expanded[at, n : n + PAIR] = b * (phi + a * density)
            expanded[at, hidden_units + n : hidden_units + n + PAIR] = gelu
        return carry

    lax.fori_loop(0, total // CHUNK, gate, 0)
    for n in range(0, width, 256):
        wide[:, n : n + 256] = nt(hid[...], wc[n : n + 256, :])

    def finish(c, carry):
        at = chunk_rows(c)
        result[at, :] = (mid[at, :] + jnp.where(valid(c), wide[at, :], 0.0)).astype(BF16)
        return carry

    lax.fori_loop(0, total // CHUNK, finish, 0)
    for n in range(0, hidden_units, 256):
        size = min(256, hidden_units - n)
        h = nn(ffn_grad[...], wc[:, n : n + size])
        exp_grad[:, n : n + size] = (h * expanded[:, n : n + size]).astype(BF16)
        exp_grad[:, hidden_units + n : hidden_units + n + size] = (
            h * expanded[:, hidden_units + n : hidden_units + n + size]
        ).astype(BF16)
    for n in range(0, width, 256):
        wide[:, n : n + 256] = nt(exp_grad[...], we[n : n + 256, :])

    def norm_back(c, carry):
        at = chunk_rows(c)
        g, h = wide[at, :], hat[at, :]
        gh = g * h
        mid_term[...] += jnp.sum(gh.reshape(CHUNK // 8, 8, width), axis=0)
        u = g * gain[...]
        mean_u = jnp.mean(u, axis=-1, keepdims=True)
        mean_uh = jnp.mean(u * h, axis=-1, keepdims=True)
        scale = jnp.concatenate([root[at, :]] * pairs, axis=1)
        m = cot[at, :].astype(F32) + (u - mean_u - h * mean_uh) * scale
        mid_grad[at, :] = m
        attn_grad[at, :] = jnp.where(valid(c), m, 0.0).astype(BF16)
        return carry

    lax.fori_loop(0, total // CHUNK, norm_back, 0)
    for n in range(0, width, 256):
        att_grad[:, n : n + 256] = nt(attn_grad[...], wp[n : n + 256, :]).astype(BF16)

    def attend_back(p, carry):
        lanes = pl.ds(pl.multiple_of(p * PAIR, PAIR), PAIR)
        for t in range(STEP_SLOTS):
            at = slice(t * rows, (t + 1) * rows)
            queries = two_heads(q[at, lanes] * jnp.asarray(HEAD_DIM**-0.5, BF16))
            grads = two_heads(att_grad[at, lanes])
            prob = probs[t, p]
            prob_grad = nt(vt[t, :, lanes], grads)
            total_grad = jnp.sum(prob * prob_grad, axis=0, keepdims=True)
            score_grad = (prob * (prob_grad - total_grad)).astype(BF16)
            tiles[1, t, :, lanes] = nn(prob.astype(BF16), grads)
            tiles[0, t, :, lanes] = nn(score_grad, queries)
            g = from_heads(tn(kt[t, :, lanes], score_grad), rows) * np.float32(HEAD_DIM**-0.5)
            c, s = slot_angles(slots[t][4], ca, sa, cb, sb)
            dq[at, lanes] = (g * c - swap_halves(g) * s).astype(BF16)
        return carry

    lax.fori_loop(0, pairs, attend_back, 0)
    for t, (slot, micro, pred, succ, _, _) in enumerate(slots):
        for which, out in ((0, dk), (1, dv)):
            part = which * half
            out[slot] += tiles[which, t, half : half + rows, :]

            @pl.when(pred < blocks)
            def _(out=out, which=which, t=t, micro=micro, pred=pred):
                out[micro * blocks + pred, half:, :] += tiles[which, t, :half, :]

            @pl.when(pred >= blocks)
            def _(part=part, which=which, t=t, micro=micro):
                back_prev[micro, part : part + half, :] = tiles[which, t, :half, :].astype(BF16)

            @pl.when(succ < blocks)
            def _(out=out, which=which, t=t, micro=micro, succ=succ):
                out[micro * blocks + succ, :half, :] += tiles[which, t, half + rows :, :]

            @pl.when(succ >= blocks)
            def _(part=part, which=which, t=t, micro=micro):
                back_next[micro, part : part + half, :] = tiles[which, t, half + rows :, :].astype(BF16)


def input_kernel(
    blocks, group, rows, width,
    lengths, dealing, dq, dk, dv, from_next, from_prev, x, mid_grad, w_all, gain, ca, sa, cb, sb,
    delta, input_grad, pre_term,
    w, wide, sem,
):
    step = pl.program_id(0)
    half = rows // 2

    @pl.when(step == 0)
    def _():
        copy = pltpu.make_async_copy(w_all.at[:, pl.ds(0, 3 * width)], w, sem)
        copy.start()
        copy.wait()
        pre_term[...] = jnp.zeros_like(pre_term)

    for t in range(STEP_SLOTS):
        micro, _, local, offset, _ = slot_scalars(lengths, dealing, step * STEP_SLOTS + t, blocks, group)
        c, s = slot_angles(offset, ca, sa, cb, sb)
        last = jnp.where(local == blocks - 1, 1.0, 0.0)
        first = jnp.where(local == 0, 1.0, 0.0)
        for top, weight, back in ((0, first, from_prev), (half, last, from_next)):
            at = slice(t * rows + top, t * rows + top + half)
            ct, st = c[top : top + half], s[top : top + half]
            for p in range(width // PAIR):
                lanes = slice(p * PAIR, (p + 1) * PAIR)
                g = dk[t, top : top + half, lanes] + weight * back[micro, :half, lanes].astype(F32)
                delta[at, lanes] = dq[at, lanes]
                delta[at, width + p * PAIR : width + (p + 1) * PAIR] = (g * ct - swap_halves(g) * st).astype(BF16)
                g = dv[t, top : top + half, lanes] + weight * back[micro, half:, lanes].astype(F32)
                delta[at, 2 * width + p * PAIR : 2 * width + (p + 1) * PAIR] = g.astype(BF16)
    for n in range(0, width, 256):
        wide[:, n : n + 256] = nt(delta[...], w[n : n + 256, :])

    def norm_back(c, carry):
        at = chunk_rows(c)
        xf = x[at, :].astype(F32)
        centred = xf - jnp.mean(xf, axis=-1, keepdims=True)
        spread = jnp.mean(centred * centred, axis=-1, keepdims=True)
        scale = lax.rsqrt(spread + norm_epsilon)
        h = centred * scale
        g = wide[at, :]
        pre_term[...] += jnp.sum((g * h).reshape(CHUNK // 8, 8, width), axis=0)
        u = g * gain[...]
        mean_u = jnp.mean(u, axis=-1, keepdims=True)
        mean_uh = jnp.mean(u * h, axis=-1, keepdims=True)
        input_grad[at, :] = (mid_grad[at, :] + (u - mean_u - h * mean_uh) * scale).astype(BF16)
        return carry

    lax.fori_loop(0, STEP_SLOTS * rows // CHUNK, norm_back, 0)


def shifted(block, axis, distance):
    devices = range(lax.axis_size(axis))
    route = [(i - distance, i) for i in devices if i - distance in devices]
    return lax.ppermute(block, axis, route)


def whole(shape):
    return pl.BlockSpec(shape, lambda i: (0,) * len(shape), pipeline_mode=pl.Buffered(1))


def by_step(shape):
    return pl.BlockSpec(shape, lambda i: (i,) + (0,) * (len(shape) - 1))


SMEM = pl.BlockSpec(memory_space=pltpu.SMEM)
ANY = pl.BlockSpec(memory_space=pl.ANY)


def local(
    inputs, cotangent, qkv_weight, proj_weight, expand_weight, contract_weight,
    prenorm, midnorm, lengths, dealing, holders, counts,
):
    micros, row_count, width = inputs.shape
    blocks = dealing.shape[1]
    rows = row_count // blocks
    hidden_units = contract_weight.shape[0]
    share = qkv_weight.shape[0]
    group = blocks * lax.axis_size("fsdp")
    slots = micros * blocks
    steps = slots // STEP_SLOTS
    total = slots * rows
    per = STEP_SLOTS * rows
    axes = ("dp", "fsdp")
    sds = jax.ShapeDtypeStruct
    tables = rope_tables(group, rows)
    table_specs = [whole(t.shape) for t in tables]
    lengths = lengths.reshape(micros, -1)
    holders = holders.reshape(micros * 2, blocks)
    x = inputs.reshape(total, width)
    cot = cotangent.reshape(total, width)

    gains = jnp.pad(jnp.stack([prenorm, midnorm], axis=1), ((0, 0), (0, PAIR - 2)))
    packed = jnp.concatenate([qkv_weight, expand_weight, contract_weight.T, proj_weight, gains], axis=1)
    w_all = lax.all_gather(packed, axes, axis=0, tiled=True)
    columns = w_all.shape[1]
    gains = w_all[:, columns - PAIR : columns - PAIR + 2].astype(F32).T
    gain_pre, gain_mid = gains[0:1], gains[1:2]
    params = functools.partial(pltpu.CompilerParams, vmem_limit_bytes=VMEM_LIMIT, dimension_semantics=("arbitrary",))

    q, k, v, normed_one, to_next, to_prev = pl.pallas_call(
        functools.partial(qkv_kernel, blocks, group, rows, width),
        grid=(steps,),
        in_specs=[SMEM] * 3 + [by_step((per, width)), ANY, whole((1, width))] + table_specs,
        out_specs=[by_step((per, width))] * 4 + [whole((micros, rows, width)), whole((micros, rows + 16, width))],
        out_shape=[sds((total, width), BF16)] * 4
        + [sds((micros, rows, width), BF16), sds((micros, rows + 16, width), BF16)],
        scratch_shapes=[
            pltpu.VMEM((width, 3 * width), BF16),
            pltpu.VMEM((per, 3 * width), F32),
            pltpu.VMEM((per, PAIR), F32),
            pltpu.VMEM((per, PAIR), F32),
            pltpu.SemaphoreType.DMA,
        ],
        compiler_params=params(),
        name="qkv",
    )(lengths, dealing, counts, x, w_all, gain_pre, *tables)

    from_prev = shifted(to_next, "fsdp", 1)
    from_next = shifted(to_prev, "fsdp", -1)

    outs = pl.pallas_call(
        functools.partial(layer_kernel, blocks, group, rows, width, hidden_units),
        grid=(steps,),
        in_specs=[SMEM] * 4
        + [by_step((per, width)), whole((slots, rows, width)), whole((slots, rows, width))]
        + [whole((micros, rows, width)), whole((micros, rows + 16, width))]
        + [by_step((per, width))] * 2
        + [ANY, whole((1, width))]
        + table_specs,
        out_specs=[by_step((per, width))] * 3
        + [by_step((per, hidden_units)), by_step((per, width)), by_step((per, width))]
        + [by_step((per, 2 * hidden_units)), by_step((per, width)), by_step((per, width))]
        + [whole((slots, rows, width))] * 2
        + [whole((micros, rows, width))] * 2
        + [whole((8, width))],
        out_shape=[
            sds((total, width), BF16),
            sds((total, width), F32),
            sds((total, width), BF16),
            sds((total, hidden_units), BF16),
            sds((total, width), BF16),
            sds((total, width), BF16),
            sds((total, 2 * hidden_units), BF16),
            sds((total, width), BF16),
            sds((total, width), BF16),
            sds((slots, rows, width), F32),
            sds((slots, rows, width), F32),
            sds((micros, rows, width), BF16),
            sds((micros, rows, width), BF16),
            sds((8, width), F32),
        ],
        scratch_shapes=[
            pltpu.VMEM((width, width), BF16),
            pltpu.VMEM((width, 2 * hidden_units), BF16),
            pltpu.VMEM((width, hidden_units), BF16),
            pltpu.VMEM((STEP_SLOTS, 2 * rows, width), BF16),
            pltpu.VMEM((STEP_SLOTS, 2 * rows, width), BF16),
            pltpu.VMEM((STEP_SLOTS, 2 * rows, rows), F32),
            pltpu.VMEM((STEP_SLOTS, width // PAIR, 2 * rows, 2 * rows), F32),
            pltpu.VMEM((per, 2 * hidden_units), F32),
            pltpu.VMEM((per, width), F32),
            pltpu.VMEM((per, width), F32),
            pltpu.VMEM((per, width), F32),
            pltpu.VMEM((per, PAIR), F32),
            pltpu.VMEM((per, width), BF16),
            pltpu.VMEM((2, STEP_SLOTS, 2 * rows, width), F32),
            pltpu.SemaphoreType.DMA((3,)),
        ],
        compiler_params=params(),
        name="layer",
    )(
        lengths, dealing, holders, counts,
        q, k.reshape(slots, rows, width), v.reshape(slots, rows, width),
        from_prev, from_next, x, cot, w_all, gain_mid, *tables,
    )
    result, mid_grad, dq, hid, ffn_grad, normed_two, exp_grad, attended, attn_grad = outs[:9]
    dk, dv, back_prev, back_next, mid_term = outs[9:]

    ret_next = shifted(back_prev, "fsdp", -1)
    ret_prev = shifted(back_next, "fsdp", 1)
    term_expand = tn(normed_two, exp_grad).astype(BF16)
    term_contract = tn(ffn_grad, hid).astype(BF16)
    term_proj = tn(attended, attn_grad).astype(BF16)

    delta, input_grad, pre_term = pl.pallas_call(
        functools.partial(input_kernel, blocks, group, rows, width),
        grid=(steps,),
        in_specs=[SMEM] * 2
        + [by_step((per, width)), by_step((STEP_SLOTS, rows, width)), by_step((STEP_SLOTS, rows, width))]
        + [whole((micros, rows, width))] * 2
        + [by_step((per, width))] * 2
        + [ANY, whole((1, width))]
        + table_specs,
        out_specs=[by_step((per, 3 * width)), by_step((per, width)), whole((8, width))],
        out_shape=[sds((total, 3 * width), BF16), sds((total, width), BF16), sds((8, width), F32)],
        scratch_shapes=[
            pltpu.VMEM((width, 3 * width), BF16),
            pltpu.VMEM((per, width), F32),
            pltpu.SemaphoreType.DMA,
        ],
        compiler_params=params(),
        name="input",
    )(lengths, dealing, dq, dk, dv, ret_next, ret_prev, x, mid_grad, w_all, gain_pre, *tables)
    term_qkv = tn(normed_one, delta).astype(BF16)

    terms = jnp.stack([jnp.sum(pre_term, axis=0), jnp.sum(mid_term, axis=0)], axis=1)
    terms = jnp.pad(terms, ((0, 0), (0, PAIR - 2))).astype(BF16)
    grads = jnp.concatenate([term_qkv, term_expand, term_contract, term_proj, terms], axis=1)
    shard = lax.psum_scatter(grads, axes, scatter_dimension=0, tiled=True).astype(F32)
    at = np.cumsum([0, 3 * width, 2 * hidden_units, hidden_units, width])
    return (
        result.reshape(inputs.shape),
        input_grad.reshape(inputs.shape),
        shard[:, at[0] : at[1]],
        shard[:, at[3] : at[4]],
        shard[:, at[1] : at[2]],
        shard[:, at[2] : at[3]].T,
        shard[:, at[4]],
        shard[:, at[4] + 1],
    )


def solution(mesh):
    both = ("dp", "fsdp")
    return jax.shard_map(
        local,
        mesh=mesh,
        in_specs=(
            P(None, both, None), P(None, both, None),
            P(both, None), P(both, None), P(both, None), P(None, both), P(both), P(both),
            P(None, "dp", None), P(None, both), P(None, None, both), P(None, both),
        ),
        out_specs=(
            P(None, both, None), P(None, both, None),
            P(both, None), P(both, None), P(both, None), P(None, both), P(both), P(both),
        ),
        check_vma=False,
    )
```

time: 823 us -> 467 us (0.57)
  local copies, waits for them, and re-layouts: 247 us -> 12.1 us
  Pallas kernels: 0 us -> 160 us
  matrix products: 165 us -> 22.4 us
  other arithmetic: 100 us -> 4.17 us
  blocking collectives: 90 us -> 0 us
  waiting for transfers between devices: 166 us -> 240 us
  starting transfers between devices: 24.5 us -> 13.6 us
  between operations: 24.3 us -> 14.2 us
    pallas_call x0 -> x3, Pallas kernels: none -> 160 us  [the longest x1 110 us: local(): pl.pallas_call(functools.partial(layer_kernel, blocks, group, rows, width...]
    dot_general x40 -> x4, matrix products: 165 us -> 22.4 us  [tn(): lax.dot_general(a, b, (((0,), (0,)), ((), ())), preferred_element_type=F32)]
    unnamed x2 -> x0, blocking collectives: 90 us -> none
    all_gather x4 -> x1, waiting for transfers between devices: 0.03 us -> 87.8 us  [local(): w_all = lax.all_gather(packed, axes, axis=0, tiled=True)]
    slice x34 -> x4, local copies, waits for them, and re-layouts: 50.4 us -> 4.44 us  [the longest x1 1.74 us: local(): shard[:, at[1]:at[2]]]
    another operation x13 -> x3, local copies, waits for them, and re-layouts: 38.7 us -> 0.2 us  [local(): jnp.stack([jnp.sum(pre_term, axis=0), jnp.sum(mid_term, axis=0)], axis=1)]
    convert_element_type x19 -> x1, other arithmetic: 37.1 us -> 1.01 us  [local(): lax.psum_scatter(grads, axes, scatter_dimension=0, tiled=True).astype(F32)]
    mul x12 -> x0, local copies, waits for them, and re-layouts: 35 us -> none  [the longest x10 29.3 us: apply_rope(): return values * cos_table + rotate_half(values) * sin_table]
  transfers between devices with their start and end apart: 18 -> 6, of which waited for: 2 -> 4; matrix products, arithmetic and copies ran while one was open for 55% -> 0% of each run, Pallas kernels for 0% -> 0%
where the time goes in v1:
time: 467 us; the launch traced here: 466 us
  waiting for transfers between devices  240 us (51%)
  Pallas kernels  160 us (34%)
  matrix products  22.4 us (5%)
  between operations  14.2 us (3%)
  starting transfers between devices  13.6 us (3%)
  local copies, waits for them, and re-layouts  12.1 us (3%)
    reduce_scatter x1, waiting for transfers between devices, local(): lax.psum_scatter(grads, axes, scatter_dimension=0, tiled=True).astype(F32)  150 us
    pallas_call x1, Pallas kernels, local(): pl.pallas_call(functools.partial(layer_kernel, blocks, group, rows, width...  110 us
    all_gather x1, waiting for transfers between devices, local(): w_all = lax.all_gather(packed, axes, axis=0, tiled=True)  87.8 us
    pallas_call x1, Pallas kernels, local(): pl.pallas_call(functools.partial(qkv_kernel, blocks, group, rows, width),...  25 us
    pallas_call x1, Pallas kernels, local(): pl.pallas_call(functools.partial(input_kernel, blocks, group, rows, width...  24.6 us
    dot_general x4, matrix products, tn(): lax.dot_general(a, b, (((0,), (0,)), ((), ())), preferred_element_type=F32)  22.4 us
    ppermute x4, starting transfers between devices, shifted(): return lax.ppermute(block, axis, route)  13.5 us
  transfers between devices with their start and end apart: 6, of which 4 were waited for; matrix products, arithmetic and copies ran while one was open for 0% of the time, Pallas kernels for 0%

profile of v1, /device:TPU:0, one launch (start us, length us, event | category | flops | bytes accessed | tf_op | source)
XLA Modules:
  0.0 466.2 jit_solution(5198167222515485943)
XLA Ops:
  7.2 0.0 all-gather.2.cloned.1.call-start
  7.2 0.7 pad_maximum_fusion.1
  7.9 0.1 copy.48
  8.0 0.9 constant_dynamic-update-slice_fusion.3
  8.9 0.9 constant_dynamic-update-slice_fusion.2
  9.8 0.8 bitcast_dynamic-update-slice_fusion
  10.6 0.8 constant_dynamic-update-slice_fusion.1
  11.4 0.7 copy-done
  12.1 0.0 all-gather.2.cloned.1.call-update
  12.2 0.0 reduce-scatter.2.cloned.1.call-start
  12.2 87.8 %all-gather.2.cloned.1.call-done.w_all = bf16[768,6656]{1,0:T(8,128)(2,1)} async-done(((bf16[24,6656]{1,0:T(8,128)(2,1)}), bf16[768,6656]{1,0:T(8,128)(2,1)}) %all-gather.2.cloned.1.call-update) | async-done | bytes 10223632 | tf_op jit(solution)/shard_map/all_gather | solution.py:457
  100.0 1.0 slice_convert_fusion
  100.9 0.1 copy.49
  101.1 0.6 fusion.5
  101.7 25.0 %qkv.1 = (bf16[1280,768]{1,0:T(8,128)(2,1)}, bf16[1280,768]{1,0:T(8,128)(2,1)}, bf16[1280,768]{1,0:T(8,128)(2,1)}, bf16[1280,768]{1,0:T(8,128)(2,1)}, bf16[2,128...) custom-call(s32[2,8]{1,0:T(2,128)} %bitcast.30, s32[2,5]{1,0:T(2,128)} %dealing.5, s32[2,5]{1,0:T(2,128)} %counts.3, ...), custom_call_target="tpu_custom_call" | custom-call | tf_op jit(solution)/shard_map/qkv/pallas_call | solution.py:463
  126.7 1.3 collective-permute-start.1
  128.0 3.1 collective-permute-start
  131.0 1.5 collective-permute-done.from_prev
  132.5 0.0 collective-permute-done.1.from_next
  132.5 0.7 copy-done.3
  133.3 0.2 copy-done.1
  133.4 109.9 %layer.1 = (bf16[1280,768]{1,0:T(8,128)(2,1)}, f32[1280,768]{1,0:T(8,128)}, bf16[1280,768]{1,0:T(8,128)(2,1)}, bf16[1280,1152]{1,0:T(8,128)(2,1)}, bf16[1280,768...) custom-call(s32[2,8]{1,0:T(2,128)} %bitcast.31, ...), custom_call_target="tpu_custom_call" | custom-call | tf_op jit(solution)/shard_map/layer/pallas_call | solution.py:484
  243.4 1.3 collective-permute-start.2
  244.7 7.9 %collective-permute-start.3 = (bf16[2,128,768]{2,1,0:T(8,128)(2,1)}, bf16[2,128,768]{2,1,0:T(8,128)(2,1)S(1)}, u32[]{:S(2)}, u32[]{:S(2)}) collective-permute-start(bf16[2,128,768]{2,1,0:T(8,128)(2,1)} %get-tuple-element.41), channel_id=1, source_target_pairs={{0,1},{1,2},{2,3},{3,4},{4,5},{5,6},{6,7},{8,9},{9,10},{10,11},{11... | collective-permute-start | bytes 1179656 | tf_op jit(solution)/shard_map/ppermute | solution.py:417
  252.6 0.8 reduce_sum.19
  253.3 0.0 collective-permute-done.2.from_next
  253.4 0.0 copy-start.2
  253.4 0.5 collective-permute-done.3.from_prev
  253.9 0.2 copy-done.2
  254.1 0.6 copy-done.4
  254.7 24.6 %input.1 = (bf16[1280,2304]{1,0:T(8,128)(2,1)}, bf16[1280,768]{1,0:T(8,128)(2,1)}, f32[8,768]{1,0:T(8,128)}) custom-call(s32[2,8]{1,0:T(2,128)} %bitcast.32, s32[2,5]{1,0:T(2,128)} %dealing.5, bf16[1280,768]{1,0:T(8,128)(2,1)} %get-tuple-element.37.dq, f32[10,128,768]{2,1,0:T(8,128)} %get-tuple-element.38.dk, f32[10,128,768]{2,1,0:T(8,128)} %get-tuple-element.39.dv, ...), custom_call_target="tpu_custom_call" | custom-call | tf_op jit(solution)/shard_map/input/pallas_call | solution.py:548
  279.3 0.8 reduce_sum.18
  280.1 0.2 copy.45
  280.3 0.0 copy-done.7
  280.3 9.1 %fusion.1 = bf16[768,6656]{1,0:T(8,128)(2,1)} fusion(bf16[1280,768]{1,0:T(8,128)(2,1)S(1)} %copy-done.7, bf16[1280,2304]{1,0:T(8,128)(2,1)} %get-tuple-element.45), kind=kOutput, calls=%fused_computation.3 | convolution fusion | flops 4531617792 | bytes 11403264 | tf_op jit(solution)/shard_map/dot_general | solution.py:32
  289.4 0.0 copy-done.11
  289.5 6.4 %fusion = bf16[768,6656]{1,0:T(8,128)(2,1)} fusion(bf16[768,6656]{1,0:T(8,128)(2,1)} %fusion.1, bf16[1280,768]{1,0:T(8,128)(2,1)S(1)} %copy-done.11, bf16[1280,2304]{1,0:T(8,128)(2,1)S(1)} %copy-done.5), kind=kOutput, calls=%fused_computation.1 | convolution fusion | flops 4531617792 | bytes 11403264 | tf_op jit(solution)/shard_map/dot_general | solution.py:32
  295.9 4.0 fusion.2
  299.9 0.0 copy-done.8
  299.9 2.9 fusion.3
  302.8 0.7 pad_dynamic-update-slice_fusion
  303.5 0.0 reduce-scatter.2.cloned.1.call-update
  303.5 150.3 %reduce-scatter.2.cloned.1.call-done = bf16[24,6656]{1,0:T(8,128)(2,1)} async-done(((bf16[768,6656]{1,0:T(8,128)(2,1)}), bf16[24,6656]{1,0:T(8,128)(2,1)}) %reduce-scatter.2.cloned.1.call-update) | async-done | bytes 319504 | tf_op jit(solution)/shard_map/reduce_scatter | solution.py:572
  453.8 1.0 convert_element_type.25
  454.9 0.7 slice_reduce_fusion
  455.6 0.7 slice_bitcast_fusion
  456.2 1.4 slice.40
  457.6 1.7 fusion.4
  (19 shorter events, 0.1 us)
Async XLA Ops:
  7.2 92.8 %all-gather.2.cloned.1.call-start = ((), (), s32[]{:S(2)}) async-start(), calls=%async_computation.1 | async-start | bytes 10543104 | tf_op jit(solution)/shard_map/all_gather | solution.py:457
  11.4 0.7 copy-start
  12.2 441.7 %reduce-scatter.2.cloned.1.call-start = ((), (), s32[]{:S(2)}) async-start(), calls=%async_computation.2 | async-start | bytes 10543104 | tf_op jit(solution)/shard_map/reduce_scatter | solution.py:572
  126.7 5.9 %collective-permute-start.1 = (bf16[2,144,768]{2,1,0:T(8,128)(2,1)}, bf16[2,144,768]{2,1,0:T(8,128)(2,1)S(1)}, u32[]{:S(2)}, u32[]{:S(2)}) collective-permute-start(bf16[2,144,768]{2,1,0:T(8,128)(2,1)} %get-tuple-element.35), channel_id=1, source_target_pairs={{1,0},{2,1},{3,2},{4,3},{5,4},{6,5},{7,6},{9,8},{10,9},{11,10},{12... | collective-permute-start | bytes 1327112 | tf_op jit(solution)/shard_map/ppermute | solution.py:417
  128.0 4.6 collective-permute-start
  132.5 0.7 copy-start.3
  132.5 0.9 copy-start.1
  243.4 10.0 %collective-permute-start.2 = (bf16[2,128,768]{2,1,0:T(8,128)(2,1)}, bf16[2,128,768]{2,1,0:T(8,128)(2,1)S(1)}, u32[]{:S(2)}, u32[]{:S(2)}) collective-permute-start(bf16[2,128,768]{2,1,0:T(8,128)(2,1)} %get-tuple-element.40), channel_id=1, source_target_pairs={{1,0},{2,1},{3,2},{4,3},{5,4},{6,5},{7,6},{9,8},{10,9},{11,10},{12... | collective-permute-start | bytes 1179656 | tf_op jit(solution)/shard_map/ppermute | solution.py:417
  244.7 9.2 %collective-permute-start.3 = (bf16[2,128,768]{2,1,0:T(8,128)(2,1)}, bf16[2,128,768]{2,1,0:T(8,128)(2,1)S(1)}, u32[]{:S(2)}, u32[]{:S(2)}) collective-permute-start(bf16[2,128,768]{2,1,0:T(8,128)(2,1)} %get-tuple-element.41), channel_id=1, source_target_pairs={{0,1},{1,2},{2,3},{3,4},{4,5},{5,6},{6,7},{8,9},{9,10},{10,11},{11... | collective-permute-start | bytes 1179656 | tf_op jit(solution)/shard_map/ppermute | solution.py:417
  253.4 0.8 copy-start.2
  253.9 0.7 copy-start.4
  254.7 25.6 %copy-start.7 = (bf16[1280,768]{1,0:T(8,128)(2,1)S(1)}, bf16[1280,768]{1,0:T(8,128)(2,1)}, u32[]{:S(2)}) copy-start(bf16[1280,768]{1,0:T(8,128)(2,1)} %get-tuple-element.44) | copy-start | bytes 5898244
  280.3 9.2 %copy-start.5 = (bf16[1280,2304]{1,0:T(8,128)(2,1)S(1)}, bf16[1280,2304]{1,0:T(8,128)(2,1)}, u32[]{:S(2)}) copy-start(bf16[1280,2304]{1,0:T(8,128)(2,1)} %get-tuple-element.47) | copy-start | bytes 17694724
  280.3 9.2 %copy-start.11 = (bf16[1280,768]{1,0:T(8,128)(2,1)S(1)}, bf16[1280,768]{1,0:T(8,128)(2,1)}, u32[]{:S(2)}) copy-start(bf16[1280,768]{1,0:T(8,128)(2,1)} %get-tuple-element.46) | copy-start | bytes 5898244
  289.4 6.4 %copy-start.6 = (bf16[1280,1152]{1,0:T(8,128)(2,1)S(1)}, bf16[1280,1152]{1,0:T(8,128)(2,1)}, u32[]{:S(2)}) copy-start(bf16[1280,1152]{1,0:T(8,128)(2,1)} %get-tuple-element.49) | copy-start | bytes 8847364
  289.5 6.4 %copy-start.10 = (bf16[1280,768]{1,0:T(8,128)(2,1)S(1)}, bf16[1280,768]{1,0:T(8,128)(2,1)}, u32[]{:S(2)}) copy-start(bf16[1280,768]{1,0:T(8,128)(2,1)} %get-tuple-element.48) | copy-start | bytes 5898244
  295.9 4.0 copy-start.8
  295.9 4.0 copy-start.9
Sparse Core Ops, SparseCore 0:
  12.3 87.6 all-gather.1
  303.6 150.1 reduce-scatter.1

commit v2 on v1

--- a/solution.py
+++ b/solution.py
@@ -429,6 +429,312 @@
 ANY = pl.BlockSpec(memory_space=pl.ANY)
 
 
+MESH = pl.DeviceIdType.MESH
+LANES = 512
+
+
+class Place:
+    def __init__(self):
+        self.nz, self.fs = lax.axis_size("dp"), lax.axis_size("fsdp")
+        self.z = lax.axis_index("dp")
+        self.f = lax.axis_index("fsdp")
+        self.c = lax.rem(self.f, 2)
+        first, second = self.f // 4, lax.rem(self.f // 2, 2)
+        self.a2 = self.c * second + (1 - self.c) * first
+        self.a3 = self.c * first + (1 - self.c) * second
+        self.s2 = 4 - 2 * self.c
+        self.s3 = 2 + 2 * self.c
+
+    def square(self, x2, x3):
+        return x2 * self.s2 + x3 * self.s3
+
+    def at(self, z=None, x2=None, x3=None, other=False):
+        z = self.z if z is None else z
+        x2 = self.a2 if x2 is None else x2
+        x3 = self.a3 if x3 is None else x3
+        c = 1 - self.c if other else self.c
+        return {"dp": z, "fsdp": self.square(x2, x3) + c}
+
+    def greet(self):
+        barrier = pltpu.get_barrier_semaphore()
+        last = self.nz - 1
+
+        def signal(device):
+            pl.semaphore_signal(barrier, inc=1, device_id=device, device_id_type=MESH)
+
+        signal(self.at(x2=1 - self.a2))
+        signal(self.at(x3=1 - self.a3))
+        signal(self.at(other=True))
+        pl.when(self.z < last)(lambda: signal(self.at(z=self.z + 1)))
+        pl.when(self.z > 0)(lambda: signal(self.at(z=self.z - 1)))
+        pl.semaphore_wait(barrier, 3 + (self.z + last) // self.nz + (2 * last - self.z) // self.nz)
+
+
+def gather_kernel(own, out, send, recv, local_sem):
+    at = Place()
+    z, nz, c = at.z, at.nz, at.c
+    at.greet()
+    started = []
+
+    def item(zz, x2, x3, core):
+        return zz * at.fs + at.square(x2, x3) + core
+
+    def copy(src, it, slot, device):
+        return pltpu.make_async_remote_copy(
+            src_ref=src, dst_ref=out.at[it], send_sem=send.at[slot, it], recv_sem=recv.at[it],
+            device_id=device, device_id_type=MESH,
+        )
+
+    def arrived(it):
+        copy(out.at[it], it, 0, at.at(other=True)).wait_recv()
+
+    def guarded(cond, fn):
+        if cond is None:
+            fn()
+        else:
+            pl.when(cond)(fn)
+
+    def handle(it, src, cond, targets):
+        def body():
+            if cond is not True:
+                arrived(it)
+            for slot, device, inner in targets:
+                guarded(inner, lambda: copy(src(), it, slot, device).start())
+
+        guarded(None if cond is True else cond, body)
+        for slot, device, inner in targets:
+            parts = [p for p in (cond, inner) if p is not None and p is not True]
+            both = functools.reduce(jnp.logical_and, parts) if parts else None
+            started.append((it, slot, device, both))
+
+    up = (0, at.at(z=z + 1), z < nz - 1)
+    down = (1, at.at(z=z - 1), z > 0)
+    over2 = (2, at.at(x2=1 - at.a2), None)
+    over3 = (3, at.at(x3=1 - at.a3), None)
+    over = (4, at.at(other=True), None)
+    a2, a3 = at.a2, at.a3
+    mine = item(z, a2, a3, c)
+    handle(mine, lambda: own, True, (over3, over2, up, down, over))
+    keep = pltpu.make_async_copy(own, out.at[mine], local_sem)
+    keep.start()
+
+    def forward(zz, x2, x3, cond, targets):
+        it = item(zz, x2, x3, c)
+        handle(it, lambda: out.at[it], cond, targets)
+
+    def third(zz, cond):
+        for x2 in (a2, 1 - a2):
+            forward(zz, x2, 1 - a3, cond, (over,))
+
+    sources = [(z, None, None)]
+    for d in range(1, nz):
+        sources.append((z - d, z - d >= 0, up))
+        sources.append((z + d, z + d < nz, down))
+    for n, (zz, cond, ahead) in enumerate(sources):
+        if ahead is not None:
+            forward(zz, a2, a3, cond, (over3, over2, ahead, over))
+        forward(zz, 1 - a2, a3, cond, (over3, over))
+        if n >= 1:
+            third(*sources[n - 1][:2])
+    third(*sources[-1][:2])
+
+    def other(n, carry):
+        arrived(2 * n + 1 - c)
+        return carry
+
+    lax.fori_loop(0, nz * at.fs // 2, other, 0)
+    keep.wait()
+    for it, slot, device, cond in started:
+        guarded(cond, lambda: copy(out.at[it], it, slot, device).wait_send())
+
+
+def gather(packed):
+    nz, fs = lax.axis_size("dp"), lax.axis_size("fsdp")
+    if fs != 8 or packed.shape[0] % 8:
+        return lax.all_gather(packed, ("dp", "fsdp"), axis=0, tiled=True)
+    devices = nz * fs
+    out = pl.pallas_call(
+        gather_kernel,
+        in_specs=[pl.BlockSpec(memory_space=pltpu.VMEM)],
+        out_specs=ANY,
+        out_shape=jax.ShapeDtypeStruct((devices, *packed.shape), packed.dtype),
+        scratch_shapes=[
+            pltpu.SemaphoreType.DMA((5, devices)),
+            pltpu.SemaphoreType.DMA((devices,)),
+            pltpu.SemaphoreType.DMA,
+        ],
+        compiler_params=pltpu.CompilerParams(collective_id=0, has_side_effects=True),
+        name="gather",
+    )(packed)
+    return out.reshape(-1, packed.shape[1])
+
+
+def reduce_kernel(
+    grads, out,
+    own, side, over3, over2, from_below, from_above,
+    own_sem, side_send, side_recv, send3, recv3, send2, recv2, send_up, recv_up, send_down, recv_down,
+):
+    at = Place()
+    z, nz, c, a2, a3 = at.z, at.nz, at.c, at.a2, at.a3
+    share, columns = out.shape
+    squares = at.fs // 2
+    at.greet()
+
+    def remote(src, dst, send, recv, device):
+        return pltpu.make_async_remote_copy(
+            src_ref=src, dst_ref=dst, send_sem=send, recv_sem=recv, device_id=device, device_id_type=MESH
+        )
+
+    def item(zz, x2, x3):
+        return zz * squares + at.square(x2, x3) // 2
+
+    sign = 1 - 2 * (z // (nz // 2))
+    order = [lax.rem(z + sign * o + nz, nz) for o in range(nz - 1, -1, -1)]
+
+    def partner_copy(i):
+        return remote(grads.at[i, 1 - c], side.at[i], side_send.at[i], side_recv.at[i], at.at(other=True))
+
+    keep = pltpu.make_async_copy(grads.at[:, c], own, own_sem)
+    keep.start()
+    for far in (1 - a2, a2):
+        for zz in order:
+            for x3 in (1 - a3, a3):
+                partner_copy(item(zz, far, x3)).start()
+    keep.wait()
+
+    def add(i, *terms):
+        def some(n, carry):
+            lanes = pl.ds(pl.multiple_of(n * LANES, LANES), LANES)
+            value = own[i, :, lanes].astype(F32)
+            for ref, j in terms:
+                value = value + ref[j, :, lanes].astype(F32)
+            own[i, :, lanes] = value.astype(BF16)
+            return carry
+
+        lax.fori_loop(0, columns // LANES, some, 0)
+
+    def copy3(i, slot):
+        return remote(own.at[i], over3.at[slot], send3.at[slot], recv3.at[slot], at.at(x3=1 - a3))
+
+    def copy2(i, k):
+        return remote(own.at[i], over2.at[k], send2.at[k], recv2.at[k], at.at(x2=1 - a2))
+
+    def copy_up(i, t):
+        return remote(own.at[i], from_below.at[t], send_up.at[t], recv_up.at[t], at.at(z=z + 1))
+
+    def copy_down(i, t):
+        return remote(own.at[i], from_above.at[t], send_down.at[t], recv_down.at[t], at.at(z=z - 1))
+
+    sent = []
+    for k, zz in enumerate(order):
+        for flag, x2 in ((1, 1 - a2), (0, a2)):
+            i = item(zz, x2, 1 - a3)
+            partner_copy(i).wait_recv()
+            add(i, (side, i))
+            one = copy3(i, 2 * k + flag)
+            one.start()
+            sent.append(one)
+
+    def third(k):
+        i = item(order[k], a2, a3)
+        copy2(i, k).wait_recv()
+        add(i, (over2, k))
+        if k < nz - 1:
+            pl.when(z == 0)(copy_up(i, order[k]).start)
+            pl.when(z == nz - 1)(copy_down(i, order[k]).start)
+
+    for k, zz in enumerate(order):
+        for flag, x2 in ((1, 1 - a2), (0, a2)):
+            i = item(zz, x2, a3)
+            partner_copy(i).wait_recv()
+            copy3(i, 2 * k + flag).wait_recv()
+            add(i, (side, i), (over3, 2 * k + flag))
+            if flag:
+                one = copy2(i, k)
+                one.start()
+                sent.append(one)
+        if k:
+            third(k - 1)
+    third(nz - 1)
+
+    def climb(t):
+        i = item(t, a2, a3)
+        copy_up(i, t).wait_recv()
+        add(i, (from_below, t))
+        copy_up(i, t).start()
+
+    def descend(t):
+        i = item(t, a2, a3)
+        copy_down(i, t).wait_recv()
+        add(i, (from_above, t))
+        copy_down(i, t).start()
+
+    for zz in range(1, nz - 1):
+
+        @pl.when(z == zz)
+        def _(zz=zz):
+            ups = [functools.partial(climb, t) for t in range(nz - 1, zz, -1)]
+            downs = [functools.partial(descend, t) for t in range(zz)]
+            for step in ups + downs if zz < nz // 2 else downs + ups:
+                step()
+
+    i = item(z, a2, a3)
+    out[...] = own[i].astype(F32)
+
+    @pl.when(z > 0)
+    def _():
+        copy_up(i, z).wait_recv()
+        out[...] += from_below[z].astype(F32)
+
+    @pl.when(z < nz - 1)
+    def _():
+        copy_down(i, z).wait_recv()
+        out[...] += from_above[z].astype(F32)
+
+    for one in sent:
+        one.wait_send()
+    for zz in range(nz):
+
+        @pl.when(z == zz)
+        def _(zz=zz):
+            for t in range(zz + 1, nz):
+                copy_up(item(t, a2, a3), t).wait_send()
+            for t in range(zz):
+                copy_down(item(t, a2, a3), t).wait_send()
+
+    def partner_done(i, carry):
+        partner_copy(i).wait_send()
+        return carry
+
+    lax.fori_loop(0, nz * squares, partner_done, 0)
+
+
+def reduce_scatter(grads, share):
+    nz, fs = lax.axis_size("dp"), lax.axis_size("fsdp")
+    if fs != 8 or share % 8 or nz % 2:
+        return lax.psum_scatter(grads, ("dp", "fsdp"), scatter_dimension=0, tiled=True).astype(F32)
+    columns = grads.shape[1]
+    items = nz * fs // 2
+    dma = pltpu.SemaphoreType.DMA
+
+    def blocks_of(n):
+        return pltpu.VMEM((n, share, columns), BF16)
+
+    return pl.pallas_call(
+        reduce_kernel,
+        in_specs=[ANY],
+        out_specs=pl.BlockSpec(memory_space=pltpu.VMEM),
+        out_shape=jax.ShapeDtypeStruct((share, columns), F32),
+        scratch_shapes=[
+            blocks_of(items), blocks_of(items), blocks_of(2 * nz), blocks_of(nz), blocks_of(nz), blocks_of(nz),
+            dma, dma((items,)), dma((items,)), dma((2 * nz,)), dma((2 * nz,)), dma((nz,)), dma((nz,)),
+            dma((nz,)), dma((nz,)), dma((nz,)), dma((nz,)),
+        ],
+        compiler_params=pltpu.CompilerParams(collective_id=1, has_side_effects=True, vmem_limit_bytes=VMEM_LIMIT),
+        name="reduce",
+    )(grads.reshape(items, 2, share, columns))
+
+
 def local(
     inputs, cotangent, qkv_weight, proj_weight, expand_weight, contract_weight,
     prenorm, midnorm, lengths, dealing, holders, counts,
@@ -443,7 +749,6 @@
     steps = slots // STEP_SLOTS
     total = slots * rows
     per = STEP_SLOTS * rows
-    axes = ("dp", "fsdp")
     sds = jax.ShapeDtypeStruct
     tables = rope_tables(group, rows)
     table_specs = [whole(t.shape) for t in tables]
@@ -454,7 +759,7 @@
 
     gains = jnp.pad(jnp.stack([prenorm, midnorm], axis=1), ((0, 0), (0, PAIR - 2)))
     packed = jnp.concatenate([qkv_weight, expand_weight, contract_weight.T, proj_weight, gains], axis=1)
-    w_all = lax.all_gather(packed, axes, axis=0, tiled=True)
+    w_all = gather(packed)
     columns = w_all.shape[1]
     gains = w_all[:, columns - PAIR : columns - PAIR + 2].astype(F32).T
     gain_pre, gain_mid = gains[0:1], gains[1:2]
@@ -569,7 +874,7 @@
     terms = jnp.stack([jnp.sum(pre_term, axis=0), jnp.sum(mid_term, axis=0)], axis=1)
     terms = jnp.pad(terms, ((0, 0), (0, PAIR - 2))).astype(BF16)
     grads = jnp.concatenate([term_qkv, term_expand, term_contract, term_proj, terms], axis=1)
-    shard = lax.psum_scatter(grads, axes, scatter_dimension=0, tiled=True).astype(F32)
+    shard = reduce_scatter(grads, share)
     at = np.cumsum([0, 3 * width, 2 * hidden_units, hidden_units, width])
     return (
         result.reshape(inputs.shape),

time: 467 us -> 357 us (0.76)
  waiting for transfers between devices: 240 us -> 2.07 us
  Pallas kernels: 160 us -> 297 us
  between operations: 14.2 us -> 0.81 us
    reduce_scatter x1 -> x0, waiting for transfers between devices: 150 us -> none  [local(): lax.psum_scatter(grads, axes, scatter_dimension=0, tiled=True).astype(F32)]
    pallas_call x0 -> x2, Pallas kernels: none -> 138 us  [the longest x1 73.2 us: reduce_scatter(): pl.pallas_call(reduce_kernel, in_specs=[ANY], out_specs=pl.BlockSpec(memo...]
    all_gather x1 -> x0, waiting for transfers between devices: 87.8 us -> none  [local(): w_all = lax.all_gather(packed, axes, axis=0, tiled=True)]
  transfers between devices with their start and end apart: 6 -> 4, of which waited for: 4 -> 2; matrix products, arithmetic and copies ran while one was open for 0% -> 0% of each run, Pallas kernels for 0% -> 0%
where the time goes in v2:
time: 357 us; the launch traced here: 354 us
  Pallas kernels  297 us (83%)
  matrix products  22.4 us (6%)
  local copies, waits for them, and re-layouts  14.1 us (4%)
  starting transfers between devices  14 us (4%)
    pallas_call x1, Pallas kernels, local(): pl.pallas_call(functools.partial(layer_kernel, blocks, group, rows, width...  110 us
    pallas_call x1, Pallas kernels, reduce_scatter(): pl.pallas_call(reduce_kernel, in_specs=[ANY], out_specs=pl.BlockSpec(memo...  73.2 us
    pallas_call x1, Pallas kernels, gather(): pl.pallas_call(gather_kernel, in_specs=[pl.BlockSpec(memory_space=pltpu.V...  64.4 us
    pallas_call x1, Pallas kernels, local(): pl.pallas_call(functools.partial(qkv_kernel, blocks, group, rows, width),...  25 us
    pallas_call x1, Pallas kernels, local(): pl.pallas_call(functools.partial(input_kernel, blocks, group, rows, width...  24.6 us
    dot_general x4, matrix products, tn(): lax.dot_general(a, b, (((0,), (0,)), ((), ())), preferred_element_type=F32)  22.4 us
    ppermute x4, starting transfers between devices, shifted(): return lax.ppermute(block, axis, route)  14 us
  transfers between devices with their start and end apart: 4, of which 2 were waited for; matrix products, arithmetic and copies ran while one was open for 0% of the time, Pallas kernels for 0%

profile of v2, /device:TPU:0, one launch (start us, length us, event | category | flops | bytes accessed | tf_op | source)
XLA Modules:
  0.0 353.7 jit_solution(3604639779036972691)
XLA Ops:
  0.6 0.7 pad_maximum_fusion.1
  1.3 0.1 copy.37
  1.4 0.9 constant_dynamic-update-slice_fusion.3
  2.3 0.9 constant_dynamic-update-slice_fusion.2
  3.2 0.8 bitcast_dynamic-update-slice_fusion
  4.1 0.8 constant_dynamic-update-slice_fusion.1
  4.8 0.7 copy-done
  5.6 64.4 %gather.1 = bf16[32,24,6656]{2,1,0:T(8,128)(2,1)} custom-call(bf16[24,6656]{1,0:T(8,128)(2,1)} %copy-done), custom_call_target="tpu_custom_call" | custom-call | tf_op jit(solution)/shard_map/gather/pallas_call | solution.py:556
  70.0 1.0 slice_convert_fusion
  70.9 0.1 copy.43
  71.1 0.6 fusion.5
  71.7 25.0 %qkv.1 = (bf16[1280,768]{1,0:T(8,128)(2,1)}, bf16[1280,768]{1,0:T(8,128)(2,1)}, bf16[1280,768]{1,0:T(8,128)(2,1)}, bf16[1280,768]{1,0:T(8,128)(2,1)}, bf16[2,128...) custom-call(s32[2,8]{1,0:T(2,128)} %bitcast.36, s32[2,5]{1,0:T(2,128)} %dealing.5, s32[2,5]{1,0:T(2,128)} %counts.3, ...), custom_call_target="tpu_custom_call" | custom-call | tf_op jit(solution)/shard_map/qkv/pallas_call | solution.py:768
  96.7 1.3 collective-permute-start.1
  98.0 3.1 collective-permute-start
  101.0 1.5 collective-permute-done.from_prev
  102.5 0.0 collective-permute-done.1.from_next
  102.5 0.7 copy-done.3
  103.3 0.2 copy-done.1
  103.5 109.9 %layer.1 = (bf16[1280,768]{1,0:T(8,128)(2,1)}, f32[1280,768]{1,0:T(8,128)}, bf16[1280,768]{1,0:T(8,128)(2,1)}, bf16[1280,1152]{1,0:T(8,128)(2,1)}, bf16[1280,768...) custom-call(s32[2,8]{1,0:T(2,128)} %bitcast.37, ...), custom_call_target="tpu_custom_call" | custom-call | tf_op jit(solution)/shard_map/layer/pallas_call | solution.py:789
  213.4 1.3 collective-permute-start.2
  214.7 8.3 %collective-permute-start.3 = (bf16[2,128,768]{2,1,0:T(8,128)(2,1)}, bf16[2,128,768]{2,1,0:T(8,128)(2,1)S(1)}, u32[]{:S(2)}, u32[]{:S(2)}) collective-permute-start(bf16[2,128,768]{2,1,0:T(8,128)(2,1)} %get-tuple-element.41), channel_id=1, source_target_pairs={{0,1},{1,2},{2,3},{3,4},{4,5},{5,6},{6,7},{8,9},{9,10},{10,11},{11... | collective-permute-start | bytes 1179656 | tf_op jit(solution)/shard_map/ppermute | solution.py:417
  223.0 0.8 reduce_sum.19
  223.8 0.0 collective-permute-done.2.from_next
  223.8 0.0 copy-start.2
  223.8 0.5 collective-permute-done.3.from_prev
  224.4 0.2 copy-done.2
  224.6 0.6 copy-done.4
  225.1 24.6 %input.1 = (bf16[1280,2304]{1,0:T(8,128)(2,1)}, bf16[1280,768]{1,0:T(8,128)(2,1)}, f32[8,768]{1,0:T(8,128)}) custom-call(s32[2,8]{1,0:T(2,128)} %bitcast.38, s32[2,5]{1,0:T(2,128)} %dealing.5, bf16[1280,768]{1,0:T(8,128)(2,1)} %get-tuple-element.37.dq, f32[10,128,768]{2,1,0:T(8,128)} %get-tuple-element.38.dk, f32[10,128,768]{2,1,0:T(8,128)} %get-tuple-element.39.dv, ...), custom_call_target="tpu_custom_call" | custom-call | tf_op jit(solution)/shard_map/input/pallas_call | solution.py:853
  249.8 0.8 reduce_sum.18
  250.6 0.2 copy.40
  250.7 0.0 copy-done.7
  250.8 0.0 copy-start.5
  250.8 0.0 copy-start.11
  250.8 9.2 %fusion.1 = bf16[768,6656]{1,0:T(8,128)(2,1)} fusion(bf16[1280,768]{1,0:T(8,128)(2,1)S(1)} %copy-done.7, bf16[1280,2304]{1,0:T(8,128)(2,1)} %get-tuple-element.45), kind=kOutput, calls=%fused_computation.3 | convolution fusion | flops 4531617792 | bytes 11403264 | tf_op jit(solution)/shard_map/dot_general | solution.py:32
  260.0 0.0 copy-done.5
  260.0 0.0 copy-done.11
  260.0 0.0 copy-start.10
  260.0 6.4 %fusion = bf16[768,6656]{1,0:T(8,128)(2,1)} fusion(bf16[768,6656]{1,0:T(8,128)(2,1)} %fusion.1, bf16[1280,768]{1,0:T(8,128)(2,1)S(1)} %copy-done.11, bf16[1280,2304]{1,0:T(8,128)(2,1)S(1)} %copy-done.5), kind=kOutput, calls=%fused_computation.1 | convolution fusion | flops 4531617792 | bytes 11403264 | tf_op jit(solution)/shard_map/dot_general | solution.py:32
  266.4 0.0 copy-done.6
  266.5 4.0 %fusion.2 = bf16[768,6656]{1,0:T(8,128)(2,1)} fusion(bf16[768,6656]{1,0:T(8,128)(2,1)} %fusion, bf16[1280,768]{1,0:T(8,128)(2,1)S(1)} %copy-done.10, bf16[1280,1152]{1,0:T(8,128)(2,1)S(1)} %copy-done.6), kind=kOutput, calls=%fused_computation.5 | convolution fusion | flops 2265808896 | bytes 6684672 | tf_op jit(solution)/shard_map/dot_general | solution.py:32
  270.4 0.0 copy-done.9
  270.4 2.8 fusion.3
  273.3 0.8 pad_dynamic-update-slice_fusion
  274.1 73.2 %reduce.5 = f32[24,6656]{1,0:T(8,128)} custom-call(bf16[16,2,24,6656]{3,2,1,0:T(8,128)(2,1)} %bitcast.13.grads), custom_call_target="tpu_custom_call" | custom-call | tf_op jit(solution)/shard_map/reduce/pallas_call | solution.py:723
  347.3 1.5 slice_reduce_fusion
  348.8 1.5 slice.31
  350.3 1.5 slice_bitcast_fusion
  351.9 1.8 fusion.4
  (14 shorter events, 0.1 us)
Async XLA Ops:
  4.8 0.7 copy-start
  96.7 5.9 %collective-permute-start.1 = (bf16[2,144,768]{2,1,0:T(8,128)(2,1)}, bf16[2,144,768]{2,1,0:T(8,128)(2,1)S(1)}, u32[]{:S(2)}, u32[]{:S(2)}) collective-permute-start(bf16[2,144,768]{2,1,0:T(8,128)(2,1)} %get-tuple-element.35), channel_id=1, source_target_pairs={{1,0},{2,1},{3,2},{4,3},{5,4},{6,5},{7,6},{9,8},{10,9},{11,10},{12... | collective-permute-start | bytes 1327112 | tf_op jit(solution)/shard_map/ppermute | solution.py:417
  98.0 4.6 %collective-permute-start = (bf16[2,128,768]{2,1,0:T(8,128)(2,1)}, bf16[2,128,768]{2,1,0:T(8,128)(2,1)S(1)}, u32[]{:S(2)}, u32[]{:S(2)}) collective-permute-start(bf16[2,128,768]{2,1,0:T(8,128)(2,1)} %get-tuple-element.34), channel_id=1, source_target_pairs={{0,1},{1,2},{2,3},{3,4},{4,5},{5,6},{6,7},{8,9},{9,10},{10,11},{11... | collective-permute-start | bytes 1179656 | tf_op jit(solution)/shard_map/ppermute | solution.py:417
  102.5 0.7 copy-start.3
  102.5 0.9 copy-start.1
  213.4 10.4 %collective-permute-start.2 = (bf16[2,128,768]{2,1,0:T(8,128)(2,1)}, bf16[2,128,768]{2,1,0:T(8,128)(2,1)S(1)}, u32[]{:S(2)}, u32[]{:S(2)}) collective-permute-start(bf16[2,128,768]{2,1,0:T(8,128)(2,1)} %get-tuple-element.40), channel_id=1, source_target_pairs={{1,0},{2,1},{3,2},{4,3},{5,4},{6,5},{7,6},{9,8},{10,9},{11,10},{12... | collective-permute-start | bytes 1179656 | tf_op jit(solution)/shard_map/ppermute | solution.py:417
  214.7 9.7 %collective-permute-start.3 = (bf16[2,128,768]{2,1,0:T(8,128)(2,1)}, bf16[2,128,768]{2,1,0:T(8,128)(2,1)S(1)}, u32[]{:S(2)}, u32[]{:S(2)}) collective-permute-start(bf16[2,128,768]{2,1,0:T(8,128)(2,1)} %get-tuple-element.41), channel_id=1, source_target_pairs={{0,1},{1,2},{2,3},{3,4},{4,5},{5,6},{6,7},{8,9},{9,10},{10,11},{11... | collective-permute-start | bytes 1179656 | tf_op jit(solution)/shard_map/ppermute | solution.py:417
  223.8 0.7 copy-start.2
  224.4 0.7 copy-start.4
  225.1 25.6 %copy-start.7 = (bf16[1280,768]{1,0:T(8,128)(2,1)S(1)}, bf16[1280,768]{1,0:T(8,128)(2,1)}, u32[]{:S(2)}) copy-start(bf16[1280,768]{1,0:T(8,128)(2,1)} %get-tuple-element.44) | copy-start | bytes 5898244
  250.8 9.2 %copy-start.5 = (bf16[1280,2304]{1,0:T(8,128)(2,1)S(1)}, bf16[1280,2304]{1,0:T(8,128)(2,1)}, u32[]{:S(2)}) copy-start(bf16[1280,2304]{1,0:T(8,128)(2,1)} %get-tuple-element.47) | copy-start | bytes 17694724
  250.8 9.2 %copy-start.11 = (bf16[1280,768]{1,0:T(8,128)(2,1)S(1)}, bf16[1280,768]{1,0:T(8,128)(2,1)}, u32[]{:S(2)}) copy-start(bf16[1280,768]{1,0:T(8,128)(2,1)} %get-tuple-element.46) | copy-start | bytes 5898244
  260.0 6.4 %copy-start.6 = (bf16[1280,1152]{1,0:T(8,128)(2,1)S(1)}, bf16[1280,1152]{1,0:T(8,128)(2,1)}, u32[]{:S(2)}) copy-start(bf16[1280,1152]{1,0:T(8,128)(2,1)} %get-tuple-element.49) | copy-start | bytes 8847364
  260.0 6.4 %copy-start.10 = (bf16[1280,768]{1,0:T(8,128)(2,1)S(1)}, bf16[1280,768]{1,0:T(8,128)(2,1)}, u32[]{:S(2)}) copy-start(bf16[1280,768]{1,0:T(8,128)(2,1)} %get-tuple-element.48) | copy-start | bytes 5898244
  266.4 4.0 %copy-start.8 = (bf16[1280,768]{1,0:T(8,128)(2,1)S(1)}, bf16[1280,768]{1,0:T(8,128)(2,1)}, u32[]{:S(2)}) copy-start(bf16[1280,768]{1,0:T(8,128)(2,1)} %get-tuple-element.50) | copy-start | bytes 5898244
  266.4 4.0 %copy-start.9 = (bf16[1280,768]{1,0:T(8,128)(2,1)S(1)}, bf16[1280,768]{1,0:T(8,128)(2,1)}, u32[]{:S(2)}) copy-start(bf16[1280,768]{1,0:T(8,128)(2,1)} %get-tuple-element.51) | copy-start | bytes 5898244

commit v3 on v2

--- a/solution.py
+++ b/solution.py
@@ -80,11 +80,17 @@
 
 def two_heads(tile):
     even, odd = head_masks(tile.dtype)
-    return jnp.concatenate([tile * even, tile * odd], axis=0)
-
-
-def from_heads(t, rows):
-    return jnp.concatenate([t[:HEAD_DIM, :rows], t[HEAD_DIM:, rows:]], axis=0).T
+    half = tile.shape[0] // 2
+    first, second = tile[:half], tile[half:]
+    return jnp.concatenate([first * even, first * odd, second * even, second * odd], axis=0)
+
+
+def from_heads(mixed):
+    turned = mixed.T
+    quarter = turned.shape[0] // 4
+    even = lax.broadcasted_iota(jnp.int32, (quarter, PAIR), 1) < HEAD_DIM
+    parts = [turned[n * quarter : (n + 1) * quarter] for n in range(4)]
+    return jnp.concatenate([jnp.where(even, parts[0], parts[1]), jnp.where(even, parts[2], parts[3])], axis=0)
 
 
 def chunk_rows(c, size=CHUNK):
@@ -158,7 +164,7 @@
     q, k, v, from_prev, from_next, x, cot, w_all, gain, ca, sa, cb, sb,
     result, mid_grad, dq, hid, ffn_grad, normed, exp_grad, attended, attn_grad,
     dk, dv, back_prev, back_next, mid_term,
-    wp, we, wc, kt, vt, bias, probs, expanded, wide, mid, hat, root, att_grad, tiles, sem,
+    wp, we, wc, kt, vt, bias, probs, prob_grad, low, expanded, wide, mid, hat, root, att_grad, tiles, sem,
 ):
     step = pl.program_id(0)
     half = rows // 2
@@ -180,6 +186,7 @@
         dk[...] = jnp.zeros_like(dk)
         dv[...] = jnp.zeros_like(dv)
         mid_term[...] = jnp.zeros_like(mid_term)
+        low[...] = jnp.zeros_like(low)
 
     slots = []
     for t in range(STEP_SLOTS):
@@ -207,33 +214,47 @@
             def _(dst=dst, part=part, t=t, micro=micro):
                 dst[t, half + rows :, :] = from_next[micro, part : part + half, :]
 
-        col = lax.broadcasted_iota(jnp.int32, (2 * rows, rows), 0)
-        row = lax.broadcasted_iota(jnp.int32, (2 * rows, rows), 1)
+        col = lax.broadcasted_iota(jnp.int32, (2 * rows, 2 * rows), 0)
+        lane = lax.broadcasted_iota(jnp.int32, (2 * rows, 2 * rows), 1)
+        row = lane // rows * half + lax.rem(lane, half)
         follow = counts[micro, lax.rem(local + 1, blocks)]
-        remote = from_next[micro, rows : rows + 1, :rows].astype(F32)
-        follow = jnp.where(succ < blocks, jnp.full((1, rows), follow, jnp.int32).astype(F32), remote)
+        remote = from_next[micro, rows : rows + 1, : 2 * rows].astype(F32)
+        follow = jnp.where(succ < blocks, jnp.full((1, 2 * rows), follow, jnp.int32).astype(F32), remote)
         follow = half + rows + jnp.minimum(follow, half)
-        ends = jnp.full((1, rows), half + count, jnp.int32).astype(F32)
+        ends = jnp.full((1, 2 * rows), half + count, jnp.int32).astype(F32)
         high = jnp.where(is_last, ends, follow)
         lowest = jnp.where(offset > 0, 0, half)
         allowed = (col >= row) & (col - row <= rows) & (col >= lowest) & (col.astype(F32) < high)
         bias[t] = jnp.where(allowed, 0.0, masked_score)
 
-    def attend(p, carry):
-        lanes = pl.ds(pl.multiple_of(p * PAIR, PAIR), PAIR)
+    scaled = jnp.asarray(HEAD_DIM**-0.5, BF16)
+    places = [(t, p) for t in range(STEP_SLOTS) for p in range(pairs)]
+
+    def lanes_of(p):
+        return slice(p * PAIR, (p + 1) * PAIR)
+
+    def queries(t, p):
+        return two_heads(q[t * rows : (t + 1) * rows, lanes_of(p)] * scaled)
+
+    for t, p in places:
+        probs[t, p] = nt(kt[t, :, lanes_of(p)], queries(t, p))
+
+    windows = [(slice(n * half, n * half + 3 * half), slice(n * PAIR, (n + 1) * PAIR)) for n in range(2)]
+
+    def soften(p, carry):
         for t in range(STEP_SLOTS):
-            at = slice(t * rows, (t + 1) * rows)
-            queries = two_heads(q[at, lanes] * jnp.asarray(HEAD_DIM**-0.5, BF16))
-            scores = nt(kt[t, :, lanes], queries)
-            scores = scores + jnp.concatenate([bias[t], bias[t]], axis=1)
-            lifted = jnp.exp(scores - jnp.max(scores, axis=0, keepdims=True))
-            prob = lifted * (1.0 / jnp.sum(lifted, axis=0, keepdims=True))
-            probs[t, p] = prob
-            mixed = tn(vt[t, :, lanes], prob.astype(BF16))
-            attended[at, lanes] = from_heads(mixed, rows).astype(BF16)
-        return carry
-
-    lax.fori_loop(0, pairs, attend, 0)
+            for cols, lanes in windows:
+                scores = probs[t, p, cols, lanes] + bias[t, cols, lanes]
+                lifted = jnp.exp(scores - jnp.max(scores, axis=0, keepdims=True))
+                prob = lifted * (1.0 / jnp.sum(lifted, axis=0, keepdims=True))
+                probs[t, p, cols, lanes] = prob
+                low[t, p, cols, lanes] = prob.astype(BF16)
+        return carry
+
+    lax.fori_loop(0, pairs, soften, 0)
+    for t, p in places:
+        mixed = tn(vt[t, :, lanes_of(p)], low[t, p])
+        attended[t * rows : (t + 1) * rows, lanes_of(p)] = from_heads(mixed).astype(BF16)
 
     @pl.when(step == 0)
     def _():
@@ -319,24 +340,28 @@
     for n in range(0, width, 256):
         att_grad[:, n : n + 256] = nt(attn_grad[...], wp[n : n + 256, :]).astype(BF16)
 
-    def attend_back(p, carry):
-        lanes = pl.ds(pl.multiple_of(p * PAIR, PAIR), PAIR)
+    def grads(t, p):
+        return two_heads(att_grad[t * rows : (t + 1) * rows, lanes_of(p)])
+
+    for t, p in places:
+        prob_grad[t, p] = nt(vt[t, :, lanes_of(p)], grads(t, p))
+        tiles[1, t, :, lanes_of(p)] = nn(low[t, p], grads(t, p))
+
+    def soften_back(p, carry):
         for t in range(STEP_SLOTS):
-            at = slice(t * rows, (t + 1) * rows)
-            queries = two_heads(q[at, lanes] * jnp.asarray(HEAD_DIM**-0.5, BF16))
-            grads = two_heads(att_grad[at, lanes])
-            prob = probs[t, p]
-            prob_grad = nt(vt[t, :, lanes], grads)
-            total_grad = jnp.sum(prob * prob_grad, axis=0, keepdims=True)
-            score_grad = (prob * (prob_grad - total_grad)).astype(BF16)
-            tiles[1, t, :, lanes] = nn(prob.astype(BF16), grads)
-            tiles[0, t, :, lanes] = nn(score_grad, queries)
-            g = from_heads(tn(kt[t, :, lanes], score_grad), rows) * np.float32(HEAD_DIM**-0.5)
-            c, s = slot_angles(slots[t][4], ca, sa, cb, sb)
-            dq[at, lanes] = (g * c - swap_halves(g) * s).astype(BF16)
-        return carry
-
-    lax.fori_loop(0, pairs, attend_back, 0)
+            for cols, lanes in windows:
+                prob, grad = probs[t, p, cols, lanes], prob_grad[t, p, cols, lanes]
+                mean = jnp.sum(prob * grad, axis=0, keepdims=True)
+                low[t, p, cols, lanes] = (prob * (grad - mean)).astype(BF16)
+        return carry
+
+    lax.fori_loop(0, pairs, soften_back, 0)
+    for t in range(STEP_SLOTS):
+        c, s = slot_angles(slots[t][4], ca, sa, cb, sb)
+        for p in range(pairs):
+            tiles[0, t, :, lanes_of(p)] = nn(low[t, p], queries(t, p))
+            g = from_heads(tn(kt[t, :, lanes_of(p)], low[t, p])) * np.float32(HEAD_DIM**-0.5)
+            dq[t * rows : (t + 1) * rows, lanes_of(p)] = (g * c - swap_halves(g) * s).astype(BF16)
     for t, (slot, micro, pred, succ, _, _) in enumerate(slots):
         for which, out in ((0, dk), (1, dv)):
             part = which * half
@@ -457,7 +482,6 @@
 
     def greet(self):
         barrier = pltpu.get_barrier_semaphore()
-        last = self.nz - 1
 
         def signal(device):
             pl.semaphore_signal(barrier, inc=1, device_id=device, device_id_type=MESH)
@@ -465,14 +489,19 @@
         signal(self.at(x2=1 - self.a2))
         signal(self.at(x3=1 - self.a3))
         signal(self.at(other=True))
-        pl.when(self.z < last)(lambda: signal(self.at(z=self.z + 1)))
-        pl.when(self.z > 0)(lambda: signal(self.at(z=self.z - 1)))
-        pl.semaphore_wait(barrier, 3 + (self.z + last) // self.nz + (2 * last - self.z) // self.nz)
-
-
-def gather_kernel(own, out, send, recv, local_sem):
+        for d in range(1, self.nz):
+            signal(self.at(z=lax.rem(self.z + d, self.nz)))
+        pl.semaphore_wait(barrier, 2 + self.nz)
+
+
+def gather_kernel(parts, *refs):
+    pieces, out, (own, send, recv, local_sem) = refs[:parts], refs[parts], refs[parts + 1 :]
     at = Place()
-    z, nz, c = at.z, at.nz, at.c
+    z, nz, c, a2, a3 = at.z, at.nz, at.c, at.a2, at.a3
+    begin = 0
+    for piece in pieces:
+        own[:, begin : begin + piece.shape[1]] = piece[...]
+        begin += piece.shape[1]
     at.greet()
     started = []
 
@@ -488,55 +517,38 @@
     def arrived(it):
         copy(out.at[it], it, 0, at.at(other=True)).wait_recv()
 
-    def guarded(cond, fn):
-        if cond is None:
-            fn()
-        else:
-            pl.when(cond)(fn)
-
-    def handle(it, src, cond, targets):
-        def body():
-            if cond is not True:
-                arrived(it)
-            for slot, device, inner in targets:
-                guarded(inner, lambda: copy(src(), it, slot, device).start())
-
-        guarded(None if cond is True else cond, body)
-        for slot, device, inner in targets:
-            parts = [p for p in (cond, inner) if p is not None and p is not True]
-            both = functools.reduce(jnp.logical_and, parts) if parts else None
-            started.append((it, slot, device, both))
-
-    up = (0, at.at(z=z + 1), z < nz - 1)
-    down = (1, at.at(z=z - 1), z > 0)
-    over2 = (2, at.at(x2=1 - at.a2), None)
-    over3 = (3, at.at(x3=1 - at.a3), None)
-    over = (4, at.at(other=True), None)
-    a2, a3 = at.a2, at.a3
+    def pass_on(src, it, targets):
+        for slot, device in targets:
+            copy(src, it, slot, device).start()
+            started.append((it, slot, device))
+
+    over = (0, at.at(other=True))
+    over2 = (1, at.at(x2=1 - a2))
+    over3 = (2, at.at(x3=1 - a3))
+    order = line_order(z, nz)
+    line = [(3 + d, at.at(z=zz)) for d, zz in enumerate(order)]
     mine = item(z, a2, a3, c)
-    handle(mine, lambda: own, True, (over3, over2, up, down, over))
+    pass_on(own, mine, [over3, over2, *line, over])
     keep = pltpu.make_async_copy(own, out.at[mine], local_sem)
     keep.start()
 
-    def forward(zz, x2, x3, cond, targets):
+    def forward(zz, x2, x3, targets):
         it = item(zz, x2, x3, c)
-        handle(it, lambda: out.at[it], cond, targets)
-
-    def third(zz, cond):
+        arrived(it)
+        pass_on(out.at[it], it, targets)
+
+    def third(zz):
         for x2 in (a2, 1 - a2):
-            forward(zz, x2, 1 - a3, cond, (over,))
-
-    sources = [(z, None, None)]
-    for d in range(1, nz):
-        sources.append((z - d, z - d >= 0, up))
-        sources.append((z + d, z + d < nz, down))
-    for n, (zz, cond, ahead) in enumerate(sources):
-        if ahead is not None:
-            forward(zz, a2, a3, cond, (over3, over2, ahead, over))
-        forward(zz, 1 - a2, a3, cond, (over3, over))
-        if n >= 1:
-            third(*sources[n - 1][:2])
-    third(*sources[-1][:2])
+            forward(zz, x2, 1 - a3, [over])
+
+    forward(z, 1 - a2, a3, [over3, over])
+    for zz in order:
+        forward(zz, a2, a3, [over3, over2, over])
+    third(z)
+    for zz in order:
+        forward(zz, 1 - a2, a3, [over3, over])
+    for zz in order:
+        third(zz)
 
     def other(n, carry):
         arrived(2 * n + 1 - c)
@@ -544,39 +556,47 @@
 
     lax.fori_loop(0, nz * at.fs // 2, other, 0)
     keep.wait()
-    for it, slot, device, cond in started:
-        guarded(cond, lambda: copy(out.at[it], it, slot, device).wait_send())
-
-
-def gather(packed):
+    for it, slot, device in started:
+        copy(out.at[it], it, slot, device).wait_send()
+
+
+def line_order(z, nz):
+    sign = 1 - 2 * (z // (nz // 2))
+    return [lax.rem(z + sign * d + nz, nz) for d in range(1, nz)]
+
+
+def gather(pieces):
     nz, fs = lax.axis_size("dp"), lax.axis_size("fsdp")
-    if fs != 8 or packed.shape[0] % 8:
-        return lax.all_gather(packed, ("dp", "fsdp"), axis=0, tiled=True)
+    rows, columns = pieces[0].shape[0], sum(piece.shape[1] for piece in pieces)
+    if fs != 8 or rows % 8 or nz % 2:
+        return lax.all_gather(jnp.concatenate(pieces, axis=1), ("dp", "fsdp"), axis=0, tiled=True)
     devices = nz * fs
     out = pl.pallas_call(
-        gather_kernel,
-        in_specs=[pl.BlockSpec(memory_space=pltpu.VMEM)],
+        functools.partial(gather_kernel, len(pieces)),
+        in_specs=[pl.BlockSpec(memory_space=pltpu.VMEM)] * len(pieces),
         out_specs=ANY,
-        out_shape=jax.ShapeDtypeStruct((devices, *packed.shape), packed.dtype),
+        out_shape=jax.ShapeDtypeStruct((devices, rows, columns), BF16),
         scratch_shapes=[
-            pltpu.SemaphoreType.DMA((5, devices)),
+            pltpu.VMEM((rows, columns), BF16),
+            pltpu.SemaphoreType.DMA((nz + 2, devices)),
             pltpu.SemaphoreType.DMA((devices,)),
             pltpu.SemaphoreType.DMA,
         ],
         compiler_params=pltpu.CompilerParams(collective_id=0, has_side_effects=True),
         name="gather",
-    )(packed)
-    return out.reshape(-1, packed.shape[1])
+    )(*pieces)
+    return out.reshape(-1, columns)
 
 
 def reduce_kernel(
-    grads, out,
-    own, side, over3, over2, from_below, from_above,
-    own_sem, side_send, side_recv, send3, recv3, send2, recv2, send_up, recv_up, send_down, recv_down,
+    cuts, grads, *refs,
 ):
+    outs, refs = refs[: len(cuts)], refs[len(cuts) :]
+    own, side, over3, over2, line = refs[:5]
+    own_sem, side_send, side_recv, send3, recv3, send2, recv2, send_z, recv_z = refs[5:]
     at = Place()
     z, nz, c, a2, a3 = at.z, at.nz, at.c, at.a2, at.a3
-    share, columns = out.shape
+    columns = own.shape[2]
     squares = at.fs // 2
     at.greet()
 
@@ -588,30 +608,26 @@
     def item(zz, x2, x3):
         return zz * squares + at.square(x2, x3) // 2
 
-    sign = 1 - 2 * (z // (nz // 2))
-    order = [lax.rem(z + sign * o + nz, nz) for o in range(nz - 1, -1, -1)]
+    order = [*reversed(line_order(z, nz)), z]
 
     def partner_copy(i):
         return remote(grads.at[i, 1 - c], side.at[i], side_send.at[i], side_recv.at[i], at.at(other=True))
 
-    keep = pltpu.make_async_copy(grads.at[:, c], own, own_sem)
-    keep.start()
     for far in (1 - a2, a2):
         for zz in order:
             for x3 in (1 - a3, a3):
                 partner_copy(item(zz, far, x3)).start()
+    keep = pltpu.make_async_copy(grads.at[:, c], own, own_sem)
+    keep.start()
     keep.wait()
 
     def add(i, *terms):
-        def some(n, carry):
-            lanes = pl.ds(pl.multiple_of(n * LANES, LANES), LANES)
+        for n in range(0, columns, LANES):
+            lanes = slice(n, n + LANES)
             value = own[i, :, lanes].astype(F32)
             for ref, j in terms:
                 value = value + ref[j, :, lanes].astype(F32)
             own[i, :, lanes] = value.astype(BF16)
-            return carry
-
-        lax.fori_loop(0, columns // LANES, some, 0)
 
     def copy3(i, slot):
         return remote(own.at[i], over3.at[slot], send3.at[slot], recv3.at[slot], at.at(x3=1 - a3))
@@ -619,29 +635,25 @@
     def copy2(i, k):
         return remote(own.at[i], over2.at[k], send2.at[k], recv2.at[k], at.at(x2=1 - a2))
 
-    def copy_up(i, t):
-        return remote(own.at[i], from_below.at[t], send_up.at[t], recv_up.at[t], at.at(z=z + 1))
-
-    def copy_down(i, t):
-        return remote(own.at[i], from_above.at[t], send_down.at[t], recv_down.at[t], at.at(z=z - 1))
-
     sent = []
+
+    def send(one):
+        one.start()
+        sent.append(one)
+
     for k, zz in enumerate(order):
         for flag, x2 in ((1, 1 - a2), (0, a2)):
             i = item(zz, x2, 1 - a3)
             partner_copy(i).wait_recv()
             add(i, (side, i))
-            one = copy3(i, 2 * k + flag)
-            one.start()
-            sent.append(one)
+            send(copy3(i, 2 * k + flag))
 
     def third(k):
         i = item(order[k], a2, a3)
         copy2(i, k).wait_recv()
         add(i, (over2, k))
         if k < nz - 1:
-            pl.when(z == 0)(copy_up(i, order[k]).start)
-            pl.when(z == nz - 1)(copy_down(i, order[k]).start)
+            send(remote(own.at[i], line.at[z], send_z.at[k], recv_z.at[z], at.at(z=order[k])))
 
     for k, zz in enumerate(order):
         for flag, x2 in ((1, 1 - a2), (0, a2)):
@@ -650,57 +662,22 @@
             copy3(i, 2 * k + flag).wait_recv()
             add(i, (side, i), (over3, 2 * k + flag))
             if flag:
-                one = copy2(i, k)
-                one.start()
-                sent.append(one)
+                send(copy2(i, k))
         if k:
             third(k - 1)
     third(nz - 1)
-
-    def climb(t):
-        i = item(t, a2, a3)
-        copy_up(i, t).wait_recv()
-        add(i, (from_below, t))
-        copy_up(i, t).start()
-
-    def descend(t):
-        i = item(t, a2, a3)
-        copy_down(i, t).wait_recv()
-        add(i, (from_above, t))
-        copy_down(i, t).start()
-
-    for zz in range(1, nz - 1):
-
-        @pl.when(z == zz)
-        def _(zz=zz):
-            ups = [functools.partial(climb, t) for t in range(nz - 1, zz, -1)]
-            downs = [functools.partial(descend, t) for t in range(zz)]
-            for step in ups + downs if zz < nz // 2 else downs + ups:
-                step()
-
     i = item(z, a2, a3)
-    out[...] = own[i].astype(F32)
-
-    @pl.when(z > 0)
-    def _():
-        copy_up(i, z).wait_recv()
-        out[...] += from_below[z].astype(F32)
-
-    @pl.when(z < nz - 1)
-    def _():
-        copy_down(i, z).wait_recv()
-        out[...] += from_above[z].astype(F32)
-
+    for zz in order[:-1]:
+        remote(own.at[i], line.at[zz], send_z.at[0], recv_z.at[zz], at.at(z=zz)).wait_recv()
+    for out, (begin, end) in zip(outs, cuts):
+        for n in range(begin, end, PAIR):
+            lanes = slice(n, n + PAIR)
+            value = own[i, :, lanes].astype(F32)
+            for zz in order[:-1]:
+                value = value + line[zz, :, lanes].astype(F32)
+            out[:, n - begin : n - begin + PAIR] = value
     for one in sent:
         one.wait_send()
-    for zz in range(nz):
-
-        @pl.when(z == zz)
-        def _(zz=zz):
-            for t in range(zz + 1, nz):
-                copy_up(item(t, a2, a3), t).wait_send()
-            for t in range(zz):
-                copy_down(item(t, a2, a3), t).wait_send()
 
     def partner_done(i, carry):
         partner_copy(i).wait_send()
@@ -709,10 +686,11 @@
     lax.fori_loop(0, nz * squares, partner_done, 0)
 
 
-def reduce_scatter(grads, share):
+def reduce_scatter(grads, share, cuts):
     nz, fs = lax.axis_size("dp"), lax.axis_size("fsdp")
     if fs != 8 or share % 8 or nz % 2:
-        return lax.psum_scatter(grads, ("dp", "fsdp"), scatter_dimension=0, tiled=True).astype(F32)
+        block = lax.psum_scatter(grads, ("dp", "fsdp"), scatter_dimension=0, tiled=True).astype(F32)
+        return [block[:, begin:end] for begin, end in cuts]
     columns = grads.shape[1]
     items = nz * fs // 2
     dma = pltpu.SemaphoreType.DMA
@@ -721,14 +699,14 @@
         return pltpu.VMEM((n, share, columns), BF16)
 
     return pl.pallas_call(
-        reduce_kernel,
+        functools.partial(reduce_kernel, cuts),
         in_specs=[ANY],
-        out_specs=pl.BlockSpec(memory_space=pltpu.VMEM),
-        out_shape=jax.ShapeDtypeStruct((share, columns), F32),
+        out_specs=[pl.BlockSpec(memory_space=pltpu.VMEM)] * len(cuts),
+        out_shape=[jax.ShapeDtypeStruct((share, end - begin), F32) for begin, end in cuts],
         scratch_shapes=[
-            blocks_of(items), blocks_of(items), blocks_of(2 * nz), blocks_of(nz), blocks_of(nz), blocks_of(nz),
+            blocks_of(items), blocks_of(items), blocks_of(2 * nz), blocks_of(nz), blocks_of(nz),
             dma, dma((items,)), dma((items,)), dma((2 * nz,)), dma((2 * nz,)), dma((nz,)), dma((nz,)),
-            dma((nz,)), dma((nz,)), dma((nz,)), dma((nz,)),
+            dma((nz,)), dma((nz,)),
         ],
         compiler_params=pltpu.CompilerParams(collective_id=1, has_side_effects=True, vmem_limit_bytes=VMEM_LIMIT),
         name="reduce",
@@ -758,8 +736,7 @@
     cot = cotangent.reshape(total, width)
 
     gains = jnp.pad(jnp.stack([prenorm, midnorm], axis=1), ((0, 0), (0, PAIR - 2)))
-    packed = jnp.concatenate([qkv_weight, expand_weight, contract_weight.T, proj_weight, gains], axis=1)
-    w_all = gather(packed)
+    w_all = gather([qkv_weight, expand_weight, contract_weight.T, proj_weight, gains])
     columns = w_all.shape[1]
     gains = w_all[:, columns - PAIR : columns - PAIR + 2].astype(F32).T
     gain_pre, gain_mid = gains[0:1], gains[1:2]
@@ -823,8 +800,10 @@
             pltpu.VMEM((width, hidden_units), BF16),
             pltpu.VMEM((STEP_SLOTS, 2 * rows, width), BF16),
             pltpu.VMEM((STEP_SLOTS, 2 * rows, width), BF16),
-            pltpu.VMEM((STEP_SLOTS, 2 * rows, rows), F32),
+            pltpu.VMEM((STEP_SLOTS, 2 * rows, 2 * rows), F32),
             pltpu.VMEM((STEP_SLOTS, width // PAIR, 2 * rows, 2 * rows), F32),
+            pltpu.VMEM((STEP_SLOTS, width // PAIR, 2 * rows, 2 * rows), F32),
+            pltpu.VMEM((STEP_SLOTS, width // PAIR, 2 * rows, 2 * rows), BF16),
             pltpu.VMEM((per, 2 * hidden_units), F32),
             pltpu.VMEM((per, width), F32),
             pltpu.VMEM((per, width), F32),
@@ -874,17 +853,17 @@
     terms = jnp.stack([jnp.sum(pre_term, axis=0), jnp.sum(mid_term, axis=0)], axis=1)
     terms = jnp.pad(terms, ((0, 0), (0, PAIR - 2))).astype(BF16)
     grads = jnp.concatenate([term_qkv, term_expand, term_contract, term_proj, terms], axis=1)
-    shard = reduce_scatter(grads, share)
-    at = np.cumsum([0, 3 * width, 2 * hidden_units, hidden_units, width])
+    at = np.cumsum([0, 3 * width, 2 * hidden_units, hidden_units, width, PAIR]).tolist()
+    qkv_sum, expand_sum, contract_sum, proj_sum, gain_sum = reduce_scatter(grads, share, list(zip(at, at[1:])))
     return (
         result.reshape(inputs.shape),
         input_grad.reshape(inputs.shape),
-        shard[:, at[0] : at[1]],
-        shard[:, at[3] : at[4]],
-        shard[:, at[1] : at[2]],
-        shard[:, at[2] : at[3]].T,
-        shard[:, at[4]],
-        shard[:, at[4] + 1],
+        qkv_sum,
+        proj_sum,
+        expand_sum,
+        contract_sum.T,
+        gain_sum[:, 0],
+        gain_sum[:, 1],
     )
 
 

time: 357 us -> 320 us (0.90)
  Pallas kernels: 297 us -> 263 us
    pallas_call x1, Pallas kernels: 110 us -> 85.9 us  [local(): pl.pallas_call(functools.partial(layer_kernel, blocks, group, rows, width...]
    pallas_call x2, Pallas kernels: 138 us -> 128 us  [the longest x1 63.9 us: reduce_scatter(): pl.pallas_call(functools.partial(reduce_kernel, cuts), in_specs=[ANY], ou...]
    unnamed x29 -> x27, local copies, waits for them, and re-layouts: 5.95 us -> 8.16 us
where the time goes in v3:
time: 320 us; the launch traced here: 318 us
  Pallas kernels  263 us (82%)
  matrix products  22.4 us (7%)
  starting transfers between devices  14.2 us (4%)
  local copies, waits for them, and re-layouts  11.9 us (4%)
    pallas_call x1, Pallas kernels, local(): pl.pallas_call(functools.partial(layer_kernel, blocks, group, rows, width...  85.9 us
    pallas_call x1, Pallas kernels, reduce_scatter(): pl.pallas_call(functools.partial(reduce_kernel, cuts), in_specs=[ANY], ou...  63.9 us
    pallas_call x1, Pallas kernels, gather(): pl.pallas_call(functools.partial(gather_kernel, len(pieces)), in_specs=[p...  63.8 us
    pallas_call x1, Pallas kernels, local(): pl.pallas_call(functools.partial(qkv_kernel, blocks, group, rows, width),...  25 us
    pallas_call x1, Pallas kernels, local(): pl.pallas_call(functools.partial(input_kernel, blocks, group, rows, width...  24.6 us
    dot_general x4, matrix products, tn(): lax.dot_general(a, b, (((0,), (0,)), ((), ())), preferred_element_type=F32)  22.4 us
    ppermute x4, starting transfers between devices, shifted(): return lax.ppermute(block, axis, route)  14.2 us
    unnamed x27, local copies, waits for them, and re-layouts  8.16 us
  transfers between devices with their start and end apart: 4, of which 2 were waited for; matrix products, arithmetic and copies ran while one was open for 0% of the time, Pallas kernels for 0%

profile of v3, /device:TPU:0, one launch (start us, length us, event | category | flops | bytes accessed | tf_op | source)
XLA Modules:
  0.0 317.7 jit_solution(1774055553315825361)
XLA Ops:
  0.6 0.7 pad_maximum_fusion.1
  1.3 0.1 copy.37
  1.4 0.6 pad.9.refs_4_
  2.0 63.8 %gather.1 = bf16[32,24,6656]{2,1,0:T(8,128)(2,1)} custom-call(bf16[24,2304]{1,0:T(8,128)(2,1)} %refs_0_.1, bf16[24,2304]{1,0:T(8,128)(2,1)} %refs_1_.1, bf16[24,1152]{1,0:T(8,128)(2,1)} %bitcast.34, bf16[24,768]{1,0:T(8,128)(2,1)} %refs_3_.1, bf16[24,128]{1,0:T(8,128)(2,1)} %pad.9.refs_4_), custom_call_target="tpu_custom_call" | custom-call | tf_op jit(solution)/shard_map/gather/pallas_call | solution.py:574
  65.8 1.0 slice_convert_fusion
  66.8 0.1 copy.43
  66.9 0.6 fusion.4
  67.6 25.0 %qkv.1 = (bf16[1280,768]{1,0:T(8,128)(2,1)}, bf16[1280,768]{1,0:T(8,128)(2,1)}, bf16[1280,768]{1,0:T(8,128)(2,1)}, bf16[1280,768]{1,0:T(8,128)(2,1)}, bf16[2,128...) custom-call(s32[2,8]{1,0:T(2,128)} %bitcast.36, s32[2,5]{1,0:T(2,128)} %dealing.5, s32[2,5]{1,0:T(2,128)} %counts.3, ...), custom_call_target="tpu_custom_call" | custom-call | tf_op jit(solution)/shard_map/qkv/pallas_call | solution.py:745
  92.5 1.3 collective-permute-start.1
  93.8 3.1 collective-permute-start
  96.9 1.5 collective-permute-done.from_prev
  98.4 0.0 copy-start.2
  98.4 0.0 collective-permute-done.1.from_next
  98.4 0.7 copy-done.2
  99.2 0.2 copy-done
  99.3 85.9 %layer.1 = (bf16[1280,768]{1,0:T(8,128)(2,1)}, f32[1280,768]{1,0:T(8,128)}, bf16[1280,768]{1,0:T(8,128)(2,1)}, bf16[1280,1152]{1,0:T(8,128)(2,1)}, bf16[1280,768...) custom-call(s32[2,8]{1,0:T(2,128)} %bitcast.37, ...), custom_call_target="tpu_custom_call" | custom-call | tf_op jit(solution)/shard_map/layer/pallas_call | solution.py:766
  185.2 1.3 collective-permute-start.2
  186.5 8.5 %collective-permute-start.3 = (bf16[2,128,768]{2,1,0:T(8,128)(2,1)}, bf16[2,128,768]{2,1,0:T(8,128)(2,1)S(1)}, u32[]{:S(2)}, u32[]{:S(2)}) collective-permute-start(bf16[2,128,768]{2,1,0:T(8,128)(2,1)} %get-tuple-element.46), channel_id=1, source_target_pairs={{0,1},{1,2},{2,3},{3,4},{4,5},{5,6},{6,7},{8,9},{9,10},{10,11},{11... | collective-permute-start | bytes 1179656 | tf_op jit(solution)/shard_map/ppermute | solution.py:442
  195.1 0.8 reduce_sum.19
  195.8 0.0 collective-permute-done.2.from_next
  195.9 0.0 copy-start.1
  195.9 0.5 collective-permute-done.3.from_prev
  196.4 0.2 copy-done.1
  196.6 0.5 copy-done.3
  197.2 24.6 %input.1 = (bf16[1280,2304]{1,0:T(8,128)(2,1)}, bf16[1280,768]{1,0:T(8,128)(2,1)}, f32[8,768]{1,0:T(8,128)}) custom-call(s32[2,8]{1,0:T(2,128)} %bitcast.38, s32[2,5]{1,0:T(2,128)} %dealing.5, bf16[1280,768]{1,0:T(8,128)(2,1)} %get-tuple-element.42.dq, f32[10,128,768]{2,1,0:T(8,128)} %get-tuple-element.43.dk, f32[10,128,768]{2,1,0:T(8,128)} %get-tuple-element.44.dv, ...), custom_call_target="tpu_custom_call" | custom-call | tf_op jit(solution)/shard_map/input/pallas_call | solution.py:832
  221.8 0.8 reduce_sum.18
  222.6 0.2 copy.40
  222.8 0.0 copy-done.6
  222.8 0.0 copy-start.4
  222.8 0.0 copy-start.10
  222.8 9.1 %fusion.1 = bf16[768,6656]{1,0:T(8,128)(2,1)} fusion(bf16[1280,768]{1,0:T(8,128)(2,1)S(1)} %copy-done.6, bf16[1280,2304]{1,0:T(8,128)(2,1)} %get-tuple-element.50), kind=kOutput, calls=%fused_computation.3 | convolution fusion | flops 4531617792 | bytes 11403264 | tf_op jit(solution)/shard_map/dot_general | solution.py:32
  231.9 0.0 copy-done.4
  231.9 0.0 copy-done.10
  232.0 0.0 copy-start.9
  232.0 6.4 %fusion = bf16[768,6656]{1,0:T(8,128)(2,1)} fusion(bf16[768,6656]{1,0:T(8,128)(2,1)} %fusion.1, bf16[1280,768]{1,0:T(8,128)(2,1)S(1)} %copy-done.10, bf16[1280,2304]{1,0:T(8,128)(2,1)S(1)} %copy-done.4), kind=kOutput, calls=%fused_computation.1 | convolution fusion | flops 4531617792 | bytes 11403264 | tf_op jit(solution)/shard_map/dot_general | solution.py:32
  238.4 0.0 copy-done.5
  238.4 0.0 copy-done.9
  238.4 4.0 %fusion.2 = bf16[768,6656]{1,0:T(8,128)(2,1)} fusion(bf16[768,6656]{1,0:T(8,128)(2,1)} %fusion, bf16[1280,768]{1,0:T(8,128)(2,1)S(1)} %copy-done.9, bf16[1280,1152]{1,0:T(8,128)(2,1)S(1)} %copy-done.5), kind=kOutput, calls=%fused_computation.5 | convolution fusion | flops 2265808896 | bytes 6684672 | tf_op jit(solution)/shard_map/dot_general | solution.py:32
  242.3 0.0 copy-done.7
  242.3 0.0 copy-done.8
  242.3 2.9 fusion.3
  245.2 0.7 pad_dynamic-update-slice_fusion
  245.9 63.9 %reduce.5 = (f32[24,2304]{1,0:T(8,128)}, f32[24,2304]{1,0:T(8,128)}, f32[24,1152]{1,0:T(8,128)}, f32[24,768]{1,0:T(8,128)}, f32[24,128]{1,0:T(8,128)}) custom-call(bf16[16,2,24,6656]{3,2,1,0:T(8,128)(2,1)} %bitcast.13.grads), custom_call_target="tpu_custom_call" | custom-call | tf_op jit(solution)/shard_map/reduce/pallas_call | solution.py:701
  309.9 1.5 slice_reduce_fusion
  311.3 1.6 copy.52
  313.0 1.5 copy.53
  314.5 1.6 copy.54
  316.1 1.5 copy.55
  (9 shorter events, 0.0 us)
Async XLA Ops:
  92.5 5.9 %collective-permute-start.1 = (bf16[2,144,768]{2,1,0:T(8,128)(2,1)}, bf16[2,144,768]{2,1,0:T(8,128)(2,1)S(1)}, u32[]{:S(2)}, u32[]{:S(2)}) collective-permute-start(bf16[2,144,768]{2,1,0:T(8,128)(2,1)} %get-tuple-element.40), channel_id=1, source_target_pairs={{1,0},{2,1},{3,2},{4,3},{5,4},{6,5},{7,6},{9,8},{10,9},{11,10},{12... | collective-permute-start | bytes 1327112 | tf_op jit(solution)/shard_map/ppermute | solution.py:442
  93.8 4.6 %collective-permute-start = (bf16[2,128,768]{2,1,0:T(8,128)(2,1)}, bf16[2,128,768]{2,1,0:T(8,128)(2,1)S(1)}, u32[]{:S(2)}, u32[]{:S(2)}) collective-permute-start(bf16[2,128,768]{2,1,0:T(8,128)(2,1)} %get-tuple-element.39), channel_id=1, source_target_pairs={{0,1},{1,2},{2,3},{3,4},{4,5},{5,6},{6,7},{8,9},{9,10},{10,11},{11... | collective-permute-start | bytes 1179656 | tf_op jit(solution)/shard_map/ppermute | solution.py:442
  98.4 0.7 copy-start.2
  98.4 0.9 copy-start
  185.2 10.6 %collective-permute-start.2 = (bf16[2,128,768]{2,1,0:T(8,128)(2,1)}, bf16[2,128,768]{2,1,0:T(8,128)(2,1)S(1)}, u32[]{:S(2)}, u32[]{:S(2)}) collective-permute-start(bf16[2,128,768]{2,1,0:T(8,128)(2,1)} %get-tuple-element.45), channel_id=1, source_target_pairs={{1,0},{2,1},{3,2},{4,3},{5,4},{6,5},{7,6},{9,8},{10,9},{11,10},{12... | collective-permute-start | bytes 1179656 | tf_op jit(solution)/shard_map/ppermute | solution.py:442
  186.5 9.9 %collective-permute-start.3 = (bf16[2,128,768]{2,1,0:T(8,128)(2,1)}, bf16[2,128,768]{2,1,0:T(8,128)(2,1)S(1)}, u32[]{:S(2)}, u32[]{:S(2)}) collective-permute-start(bf16[2,128,768]{2,1,0:T(8,128)(2,1)} %get-tuple-element.46), channel_id=1, source_target_pairs={{0,1},{1,2},{2,3},{3,4},{4,5},{5,6},{6,7},{8,9},{9,10},{10,11},{11... | collective-permute-start | bytes 1179656 | tf_op jit(solution)/shard_map/ppermute | solution.py:442
  195.9 0.7 copy-start.1
  196.4 0.7 copy-start.3
  197.2 25.6 %copy-start.6 = (bf16[1280,768]{1,0:T(8,128)(2,1)S(1)}, bf16[1280,768]{1,0:T(8,128)(2,1)}, u32[]{:S(2)}) copy-start(bf16[1280,768]{1,0:T(8,128)(2,1)} %get-tuple-element.49) | copy-start | bytes 5898244
  222.8 9.2 %copy-start.4 = (bf16[1280,2304]{1,0:T(8,128)(2,1)S(1)}, bf16[1280,2304]{1,0:T(8,128)(2,1)}, u32[]{:S(2)}) copy-start(bf16[1280,2304]{1,0:T(8,128)(2,1)} %get-tuple-element.52) | copy-start | bytes 17694724
  222.8 9.2 %copy-start.10 = (bf16[1280,768]{1,0:T(8,128)(2,1)S(1)}, bf16[1280,768]{1,0:T(8,128)(2,1)}, u32[]{:S(2)}) copy-start(bf16[1280,768]{1,0:T(8,128)(2,1)} %get-tuple-element.51) | copy-start | bytes 5898244
  232.0 6.4 %copy-start.5 = (bf16[1280,1152]{1,0:T(8,128)(2,1)S(1)}, bf16[1280,1152]{1,0:T(8,128)(2,1)}, u32[]{:S(2)}) copy-start(bf16[1280,1152]{1,0:T(8,128)(2,1)} %get-tuple-element.54) | copy-start | bytes 8847364
  232.0 6.4 %copy-start.9 = (bf16[1280,768]{1,0:T(8,128)(2,1)S(1)}, bf16[1280,768]{1,0:T(8,128)(2,1)}, u32[]{:S(2)}) copy-start(bf16[1280,768]{1,0:T(8,128)(2,1)} %get-tuple-element.53) | copy-start | bytes 5898244
  238.4 4.0 %copy-start.7 = (bf16[1280,768]{1,0:T(8,128)(2,1)S(1)}, bf16[1280,768]{1,0:T(8,128)(2,1)}, u32[]{:S(2)}) copy-start(bf16[1280,768]{1,0:T(8,128)(2,1)} %get-tuple-element.55) | copy-start | bytes 5898244
  238.4 4.0 %copy-start.8 = (bf16[1280,768]{1,0:T(8,128)(2,1)S(1)}, bf16[1280,768]{1,0:T(8,128)(2,1)}, u32[]{:S(2)}) copy-start(bf16[1280,768]{1,0:T(8,128)(2,1)} %get-tuple-element.56) | copy-start | bytes 5898244

commit v4 on v3

--- a/solution.py
+++ b/solution.py
@@ -93,6 +93,11 @@
     return jnp.concatenate([jnp.where(even, parts[0], parts[1]), jnp.where(even, parts[2], parts[3])], axis=0)
 
 
+def turned(out, ref):
+    for n in range(0, ref.shape[1], PAIR):
+        out[n : n + PAIR, :] = ref[:, n : n + PAIR].T
+
+
 def chunk_rows(c, size=CHUNK):
     return pl.ds(pl.multiple_of(c * size, size), size)
 
@@ -100,8 +105,8 @@
 def qkv_kernel(
     blocks, group, rows, width,
     lengths, dealing, counts, x, w_all, gain, ca, sa, cb, sb,
-    q, k, v, normed, to_next, to_prev,
-    w, full, cos, sin, sem,
+    q, k, v, normed_t, to_next, to_prev,
+    w, full, cos, sin, normed, sem,
 ):
     step = pl.program_id(0)
     half = rows // 2
@@ -127,6 +132,7 @@
         return carry
 
     lax.fori_loop(0, STEP_SLOTS * rows // CHUNK, norm, 0)
+    turned(normed_t, normed)
     for n in range(0, 3 * width, 256):
         full[:, n : n + 256] = nn(normed[...], w[:, n : n + 256])
 
@@ -162,9 +168,9 @@
     blocks, group, rows, width, hidden_units,
     lengths, dealing, holders, counts,
     q, k, v, from_prev, from_next, x, cot, w_all, gain, ca, sa, cb, sb,
-    result, mid_grad, dq, hid, ffn_grad, normed, exp_grad, attended, attn_grad,
+    result, mid_grad, dq, hid, ffn_grad_t, normed_t, exp_grad, attended_t, attn_grad,
     dk, dv, back_prev, back_next, mid_term,
-    wp, we, wc, kt, vt, bias, probs, prob_grad, low, expanded, wide, mid, hat, root, att_grad, tiles, sem,
+    ffn_grad, normed, attended, wp, we, wc, kt, vt, bias, probs, prob_grad, low, expanded, wide, mid, hat, root, att_grad, tiles, sem,
 ):
     step = pl.program_id(0)
     half = rows // 2
@@ -286,6 +292,9 @@
         return carry
 
     lax.fori_loop(0, total // CHUNK, mid_norm, 0)
+    turned(normed_t, normed)
+    turned(ffn_grad_t, ffn_grad)
+    turned(attended_t, attended)
     for n in range(0, 2 * hidden_units, 256):
         expanded[:, n : n + 256] = nn(normed[...], we[:, n : n + 256])
 
@@ -450,7 +459,12 @@
     return pl.BlockSpec(shape, lambda i: (i,) + (0,) * (len(shape) - 1))
 
 
+def by_column(shape):
+    return pl.BlockSpec(shape, lambda i: (0, i))
+
+
 SMEM = pl.BlockSpec(memory_space=pltpu.SMEM)
+VMEM = pl.BlockSpec(memory_space=pltpu.VMEM)
 ANY = pl.BlockSpec(memory_space=pl.ANY)
 
 
@@ -480,7 +494,7 @@
         c = 1 - self.c if other else self.c
         return {"dp": z, "fsdp": self.square(x2, x3) + c}
 
-    def greet(self):
+    def greet(self, along=False):
         barrier = pltpu.get_barrier_semaphore()
 
         def signal(device):
@@ -491,7 +505,13 @@
         signal(self.at(other=True))
         for d in range(1, self.nz):
             signal(self.at(z=lax.rem(self.z + d, self.nz)))
-        pl.semaphore_wait(barrier, 2 + self.nz)
+        count = 2 + self.nz
+        if along:
+            last = self.fs - 1
+            pl.when(self.f > 0)(lambda: signal({"dp": self.z, "fsdp": self.f - 1}))
+            pl.when(self.f < last)(lambda: signal({"dp": self.z, "fsdp": self.f + 1}))
+            count = count + (self.f + last) // self.fs + (2 * last - self.f) // self.fs
+        pl.semaphore_wait(barrier, count)
 
 
 def gather_kernel(parts, *refs):
@@ -588,129 +608,317 @@
     return out.reshape(-1, columns)
 
 
-def reduce_kernel(
-    cuts, grads, *refs,
+def tail_kernel(
+    cuts, blocks, group, rows,
+    lengths, dealing, gain, ca, sa, cb, sb, mid_term, back_prev, back_next,
+    dq, dk, dv, x, mid_grad, w_all, normed_one_t, normed_two_t, ffn_grad_t, attended_t, exp_grad, hid, attn_grad,
+    input_grad, *refs,
 ):
     outs, refs = refs[: len(cuts)], refs[len(cuts) :]
-    own, side, over3, over2, line = refs[:5]
-    own_sem, side_send, side_recv, send3, recv3, send2, recv2, send_z, recv_z = refs[5:]
+    grads, side, over3, over2, line, from_next, from_prev = refs[:7]
+    n2, fg, att, eg, hd, ag, w, n1, wide, pre_term, dqs, dks, dvs, xs, mids, done = refs[7:23]
+    load_sem, step_sem, done_sem, halo_send, halo_recv = refs[23:28]
+    side_send, side_recv, send3, recv3, send2, recv2, send_z, recv_z = refs[28:]
     at = Place()
-    z, nz, c, a2, a3 = at.z, at.nz, at.c, at.a2, at.a3
-    columns = own.shape[2]
-    squares = at.fs // 2
-    at.greet()
+    z, nz, c, a2, a3, f, fs = at.z, at.nz, at.c, at.a2, at.a3, at.f, at.fs
+    share = grads.shape[2]
+    width = x.shape[1]
+    half = rows // 2
+    per = STEP_SLOTS * rows
+    steps = x.shape[0] // per
+    at.greet(along=True)
+
+    loads = [(normed_two_t, n2), (exp_grad, eg), (ffn_grad_t, fg), (hid, hd), (attended_t, att), (attn_grad, ag)]
+    loads += [(w_all.at[:, pl.ds(0, 3 * width)], w), (normed_one_t, n1)]
+    loads = [pltpu.make_async_copy(src, dst, load_sem.at[n]) for n, (src, dst) in enumerate(loads)]
 
     def remote(src, dst, send, recv, device):
         return pltpu.make_async_remote_copy(
             src_ref=src, dst_ref=dst, send_sem=send, recv_sem=recv, device_id=device, device_id_type=MESH
         )
 
-    def item(zz, x2, x3):
-        return zz * squares + at.square(x2, x3) // 2
-
+    loads[0].start()
+    loads[1].start()
+    halo_down = remote(back_prev, from_next, halo_send.at[0], halo_recv.at[0], {"dp": z, "fsdp": f - 1})
+    halo_up = remote(back_next, from_prev, halo_send.at[1], halo_recv.at[1], {"dp": z, "fsdp": f + 1})
+    pl.when(f > 0)(halo_down.start)
+    pl.when(f < fs - 1)(halo_up.start)
+    for one in loads[2:]:
+        one.start()
+
+    def step_loads(i):
+        n = i % 2
+        srcs = [
+            (dq.at[pl.ds(i * per, per)], dqs), (dk.at[pl.ds(i * STEP_SLOTS, STEP_SLOTS)], dks),
+            (dv.at[pl.ds(i * STEP_SLOTS, STEP_SLOTS)], dvs), (x.at[pl.ds(i * per, per)], xs),
+            (mid_grad.at[pl.ds(i * per, per)], mids),
+        ]
+        return [pltpu.make_async_copy(src, dst.at[n], step_sem.at[n, m]) for m, (src, dst) in enumerate(srcs)]
+
+    for one in step_loads(0):
+        one.start()
     order = [*reversed(line_order(z, nz)), z]
-
-    def partner_copy(i):
-        return remote(grads.at[i, 1 - c], side.at[i], side_send.at[i], side_recv.at[i], at.at(other=True))
-
-    for far in (1 - a2, a2):
-        for zz in order:
-            for x3 in (1 - a3, a3):
-                partner_copy(item(zz, far, x3)).start()
-    keep = pltpu.make_async_copy(grads.at[:, c], own, own_sem)
-    keep.start()
-    keep.wait()
-
-    def add(i, *terms):
-        for n in range(0, columns, LANES):
-            lanes = slice(n, n + LANES)
-            value = own[i, :, lanes].astype(F32)
-            for ref, j in terms:
-                value = value + ref[j, :, lanes].astype(F32)
-            own[i, :, lanes] = value.astype(BF16)
-
-    def copy3(i, slot):
-        return remote(own.at[i], over3.at[slot], send3.at[slot], recv3.at[slot], at.at(x3=1 - a3))
-
-    def copy2(i, k):
-        return remote(own.at[i], over2.at[k], send2.at[k], recv2.at[k], at.at(x2=1 - a2))
-
     sent = []
 
     def send(one):
         one.start()
         sent.append(one)
 
-    for k, zz in enumerate(order):
-        for flag, x2 in ((1, 1 - a2), (0, a2)):
-            i = item(zz, x2, 1 - a3)
-            partner_copy(i).wait_recv()
-            add(i, (side, i))
-            send(copy3(i, 2 * k + flag))
-
-    def third(k):
-        i = item(order[k], a2, a3)
-        copy2(i, k).wait_recv()
-        add(i, (over2, k))
-        if k < nz - 1:
-            send(remote(own.at[i], line.at[z], send_z.at[k], recv_z.at[z], at.at(z=order[k])))
-
-    for k, zz in enumerate(order):
-        for flag, x2 in ((1, 1 - a2), (0, a2)):
-            i = item(zz, x2, a3)
-            partner_copy(i).wait_recv()
-            copy3(i, 2 * k + flag).wait_recv()
-            add(i, (side, i), (over3, 2 * k + flag))
-            if flag:
-                send(copy2(i, k))
+    class Part:
+        def __init__(self, n, begin, end):
+            self.n, self.cols, self.begin, self.end = n, slice(begin, end), begin, end
+
+        def mine(self, zz, x2, x3):
+            return grads.at[zz, at.square(x2, x3) + c, :, self.cols]
+
+        def partner(self, zz, x2, x3):
+            sq = at.square(x2, x3)
+            i = zz * (fs // 2) + sq // 2
+            return remote(
+                grads.at[zz, sq + 1 - c, :, self.cols], side.at[i, :, self.cols],
+                side_send.at[self.n, i], side_recv.at[self.n, i], at.at(other=True),
+            )
+
+        def copy3(self, k, flag):
+            x2 = 1 - a2 if flag else a2
+            j = 2 * k + flag
+            return remote(
+                self.mine(order[k], x2, 1 - a3), over3.at[j, :, self.cols],
+                send3.at[self.n, j], recv3.at[self.n, j], at.at(x3=1 - a3),
+            )
+
+        def copy2(self, k):
+            return remote(
+                self.mine(order[k], 1 - a2, a3), over2.at[k, :, self.cols],
+                send2.at[self.n, k], recv2.at[self.n, k], at.at(x2=1 - a2),
+            )
+
+        def copy_z(self, k, source, target):
+            return remote(
+                self.mine(target, a2, a3), line.at[source, :, self.cols],
+                send_z.at[self.n, k], recv_z.at[self.n, source], at.at(z=target),
+            )
+
+        def add(self, zz, x2, x3, *terms):
+            mine = at.square(x2, x3) + c
+            for n in range(self.begin, self.end, LANES):
+                lanes = slice(n, min(n + LANES, self.end))
+                value = grads[zz, mine, :, lanes].astype(F32)
+                for ref, j in terms:
+                    value = value + ref[j, :, lanes].astype(F32)
+                grads[zz, mine, :, lanes] = value.astype(BF16)
+
+        def side_of(self, zz, x2, x3):
+            return side, zz * (fs // 2) + at.square(x2, x3) // 2
+
+        def put(self, k):
+            for far in (1 - a2, a2):
+                for x3 in (1 - a3, a3):
+                    send(self.partner(order[k], far, x3))
+
+        def first(self, k):
+            zz = order[k]
+            for flag, x2 in ((1, 1 - a2), (0, a2)):
+                self.partner(zz, x2, 1 - a3).wait_recv()
+                self.add(zz, x2, 1 - a3, self.side_of(zz, x2, 1 - a3))
+                send(self.copy3(k, flag))
+
+        def second(self, k):
+            zz = order[k]
+            for flag, x2 in ((1, 1 - a2), (0, a2)):
+                self.partner(zz, x2, a3).wait_recv()
+                self.copy3(k, flag).wait_recv()
+                self.add(zz, x2, a3, self.side_of(zz, x2, a3), (over3, 2 * k + flag))
+                if flag:
+                    send(self.copy2(k))
+
+        def third(self, k):
+            self.copy2(k).wait_recv()
+            self.add(order[k], a2, a3, (over2, k))
+            if k < nz - 1:
+                send(self.copy_z(k, z, order[k]))
+
+        def finish(self):
+            for zz in order[:-1]:
+                self.copy_z(0, zz, z).wait_recv()
+            mine = at.square(a2, a3) + c
+            for out, (begin, end) in zip(outs, cuts):
+                if begin < self.begin or end > self.end:
+                    continue
+                for n in range(begin, end, PAIR):
+                    lanes = slice(n, n + PAIR)
+                    value = grads[z, mine, :, lanes].astype(F32)
+                    for zz in order[:-1]:
+                        value = value + line[zz, :, lanes].astype(F32)
+                    out[:, n - begin : n - begin + PAIR] = value
+
+    def product(k, lhs, rhs, begin):
+        block = lhs[pl.ds(pl.multiple_of(order[k] * (fs * share), 16), fs * share), :]
+        columns = rhs.shape[1]
+        for n in range(0, columns, 256):
+            size = min(256, columns - n)
+            value = nn(block, rhs[:, n : n + size]).astype(BF16)
+            grads[order[k], :, :, begin + n : begin + n + size] = value.reshape(fs, share, size)
+
+    early = Part(0, cuts[0][0], cuts[2][1])
+    late = Part(1, cuts[3][0], cuts[4][1])
+
+    def early_block(k):
+        for n, (lhs, rhs) in enumerate(((n2, eg), (fg, hd), (att, ag))):
+            if k == 0:
+                loads[2 * n].wait()
+                loads[2 * n + 1].wait()
+            product(k, lhs, rhs, cuts[n][0])
+        early.put(k)
+
+    delta = eg
+
+    def write_back(i):
+        return pltpu.make_async_copy(done.at[i % 2], input_grad.at[pl.ds(i * per, per)], done_sem.at[i % 2])
+
+    def input_step(i):
+        n = i % 2
+        for one in step_loads(i):
+            one.wait()
+        if i + 1 < steps:
+            for one in step_loads(i + 1):
+                one.start()
+        base = i * per
+        for t in range(STEP_SLOTS):
+            micro, _, local, offset, _ = slot_scalars(lengths, dealing, i * STEP_SLOTS + t, blocks, group)
+            micro = (i * STEP_SLOTS + t) // blocks
+            co, si = slot_angles(offset, ca, sa, cb, sb)
+            last = jnp.where(local == blocks - 1, 1.0, 0.0)
+            head = jnp.where(local == 0, 1.0, 0.0)
+            for top, weight, back in ((0, head, from_prev), (half, last, from_next)):
+                rows_in = slice(t * rows + top, t * rows + top + half)
+                rows_out = slice(base + t * rows + top, base + t * rows + top + half)
+                ct, st = co[top : top + half], si[top : top + half]
+                for p in range(width // PAIR):
+                    lanes = slice(p * PAIR, (p + 1) * PAIR)
+                    g = dks[n, t, top : top + half, lanes] + weight * back[micro, :half, lanes].astype(F32)
+                    delta[rows_out, lanes] = dqs[n, rows_in, lanes]
+                    delta[rows_out, width + p * PAIR : width + (p + 1) * PAIR] = (
+                        g * ct - swap_halves(g) * st
+                    ).astype(BF16)
+                    g = dvs[n, t, top : top + half, lanes] + weight * back[micro, half:, lanes].astype(F32)
+                    delta[rows_out, 2 * width + p * PAIR : 2 * width + (p + 1) * PAIR] = g.astype(BF16)
+        for m in range(0, width, 256):
+            wide[:, m : m + 256] = nt(delta[base : base + per, :], w[m : m + 256, :])
+        if i >= 2:
+            write_back(i - 2).wait()
+
+        def norm_back(j, carry):
+            rows_at = chunk_rows(j)
+            xf = xs[n, rows_at, :].astype(F32)
+            centred = xf - jnp.mean(xf, axis=-1, keepdims=True)
+            spread = jnp.mean(centred * centred, axis=-1, keepdims=True)
+            scale = lax.rsqrt(spread + norm_epsilon)
+            h = centred * scale
+            g = wide[rows_at, :]
+            pre_term[...] += jnp.sum((g * h).reshape(CHUNK // 8, 8, width), axis=0)
+            u = g * gain[...]
+            mean_u = jnp.mean(u, axis=-1, keepdims=True)
+            mean_uh = jnp.mean(u * h, axis=-1, keepdims=True)
+            done[n, rows_at, :] = (mids[n, rows_at, :] + (u - mean_u - h * mean_uh) * scale).astype(BF16)
+            return carry
+
+        lax.fori_loop(0, per // CHUNK, norm_back, 0)
+        write_back(i).start()
+
+    pre_term[...] = jnp.zeros_like(pre_term)
+
+    @pl.when(f == fs - 1)
+    def _():
+        from_next[...] = jnp.zeros_like(from_next)
+
+    @pl.when(f == 0)
+    def _():
+        from_prev[...] = jnp.zeros_like(from_prev)
+
+    def halos():
+        pl.when(f < fs - 1)(halo_down.wait_recv)
+        pl.when(f > 0)(halo_up.wait_recv)
+        loads[6].wait()
+
+    work = [functools.partial(early_block, k) for k in range(nz)]
+    work += [halos, *[functools.partial(input_step, i) for i in range(steps)]]
+    stages = [[] for _ in work]
+    for k in range(nz):
+        stages[k + 1].append(functools.partial(early.first, k))
+        for lag, stage in ((2, early.second), (3, early.third)):
+            stages[k + lag].append(functools.partial(stage, k))
+    stages[min(nz + 3, len(work) - 1)].append(early.finish)
+    for one, then in zip(work, stages):
+        one()
+        for stage in then:
+            stage()
+
+    loads[7].wait()
+    row = lax.broadcasted_iota(jnp.int32, (PAIR, width), 0)
+    pre_sum = jnp.sum(pre_term[...], axis=0, keepdims=True)
+    mid_sum = jnp.sum(mid_term[...], axis=0, keepdims=True)
+    terms = jnp.where(row == 0, pre_sum, jnp.where(row == 1, mid_sum, 0.0))
+    grads[:, :, :, cuts[4][0] : cuts[4][1]] = terms.T.astype(BF16).reshape(nz, fs, share, PAIR)
+    for k in range(nz):
+        product(k, n1, delta, cuts[3][0])
+        late.put(k)
         if k:
-            third(k - 1)
-    third(nz - 1)
-    i = item(z, a2, a3)
-    for zz in order[:-1]:
-        remote(own.at[i], line.at[zz], send_z.at[0], recv_z.at[zz], at.at(z=zz)).wait_recv()
-    for out, (begin, end) in zip(outs, cuts):
-        for n in range(begin, end, PAIR):
-            lanes = slice(n, n + PAIR)
-            value = own[i, :, lanes].astype(F32)
-            for zz in order[:-1]:
-                value = value + line[zz, :, lanes].astype(F32)
-            out[:, n - begin : n - begin + PAIR] = value
+            late.first(k - 1)
+    late.first(nz - 1)
+    for k in range(nz):
+        late.second(k)
+        if k:
+            late.third(k - 1)
+    late.third(nz - 1)
+    late.finish()
     for one in sent:
         one.wait_send()
-
-    def partner_done(i, carry):
-        partner_copy(i).wait_send()
-        return carry
-
-    lax.fori_loop(0, nz * squares, partner_done, 0)
-
-
-def reduce_scatter(grads, share, cuts):
+    pl.when(f > 0)(halo_down.wait_send)
+    pl.when(f < fs - 1)(halo_up.wait_send)
+    for i in range(max(steps - 2, 0), steps):
+        write_back(i).wait()
+
+
+def tail(
+    cuts, blocks, group, rows, share, lengths, dealing, gain, tables, mid_term, back_prev, back_next,
+    dq, dk, dv, x, mid_grad, w_all, *operands,
+):
     nz, fs = lax.axis_size("dp"), lax.axis_size("fsdp")
-    if fs != 8 or share % 8 or nz % 2:
-        block = lax.psum_scatter(grads, ("dp", "fsdp"), scatter_dimension=0, tiled=True).astype(F32)
-        return [block[:, begin:end] for begin, end in cuts]
-    columns = grads.shape[1]
+    total, width = x.shape
+    per = STEP_SLOTS * rows
+    columns = cuts[-1][1]
     items = nz * fs // 2
     dma = pltpu.SemaphoreType.DMA
 
     def blocks_of(n):
         return pltpu.VMEM((n, share, columns), BF16)
 
+    def like(a):
+        return pltpu.VMEM(a.shape, a.dtype)
+
+    n1, n2, fg, att, eg, hid, ag = operands
     return pl.pallas_call(
-        functools.partial(reduce_kernel, cuts),
-        in_specs=[ANY],
-        out_specs=[pl.BlockSpec(memory_space=pltpu.VMEM)] * len(cuts),
-        out_shape=[jax.ShapeDtypeStruct((share, end - begin), F32) for begin, end in cuts],
+        functools.partial(tail_kernel, cuts, blocks, group, rows),
+        in_specs=[SMEM] * 2 + [VMEM] * 6 + [ANY] * (8 + len(operands)),
+        out_specs=[ANY] + [VMEM] * len(cuts),
+        out_shape=[jax.ShapeDtypeStruct((total, width), BF16)]
+        + [jax.ShapeDtypeStruct((share, end - begin), F32) for begin, end in cuts],
         scratch_shapes=[
-            blocks_of(items), blocks_of(items), blocks_of(2 * nz), blocks_of(nz), blocks_of(nz),
-            dma, dma((items,)), dma((items,)), dma((2 * nz,)), dma((2 * nz,)), dma((nz,)), dma((nz,)),
-            dma((nz,)), dma((nz,)),
+            pltpu.VMEM((nz, fs, share, columns), BF16),
+            blocks_of(items), blocks_of(2 * nz), blocks_of(nz), blocks_of(nz), like(back_prev), like(back_prev),
+            like(n2), like(fg), like(att), like(eg), like(hid), like(ag),
+            pltpu.VMEM((width, 3 * width), BF16), like(n1), pltpu.VMEM((per, width), F32), pltpu.VMEM((8, width), F32),
+            pltpu.VMEM((2, per, width), BF16), pltpu.VMEM((2, STEP_SLOTS, rows, width), F32),
+            pltpu.VMEM((2, STEP_SLOTS, rows, width), F32), pltpu.VMEM((2, per, width), BF16),
+            pltpu.VMEM((2, per, width), F32), pltpu.VMEM((2, per, width), BF16),
+            dma((8,)), dma((2, 5)), dma((2,)), dma((2,)), dma((2,)),
+            dma((2, items)), dma((2, items)), dma((2, 2 * nz)), dma((2, 2 * nz)), dma((2, nz)), dma((2, nz)),
+            dma((2, nz)), dma((2, nz)),
         ],
         compiler_params=pltpu.CompilerParams(collective_id=1, has_side_effects=True, vmem_limit_bytes=VMEM_LIMIT),
-        name="reduce",
-    )(grads.reshape(items, 2, share, columns))
+        name="tail",
+    )(lengths, dealing, gain, *tables, mid_term, back_prev, back_next, dq, dk, dv, x, mid_grad, w_all, *operands)
 
 
 def local(
@@ -742,18 +950,21 @@
     gain_pre, gain_mid = gains[0:1], gains[1:2]
     params = functools.partial(pltpu.CompilerParams, vmem_limit_bytes=VMEM_LIMIT, dimension_semantics=("arbitrary",))
 
-    q, k, v, normed_one, to_next, to_prev = pl.pallas_call(
+    q, k, v, normed_one_t, to_next, to_prev = pl.pallas_call(
         functools.partial(qkv_kernel, blocks, group, rows, width),
         grid=(steps,),
         in_specs=[SMEM] * 3 + [by_step((per, width)), ANY, whole((1, width))] + table_specs,
-        out_specs=[by_step((per, width))] * 4 + [whole((micros, rows, width)), whole((micros, rows + 16, width))],
-        out_shape=[sds((total, width), BF16)] * 4
+        out_specs=[by_step((per, width))] * 3
+        + [by_column((width, per)), whole((micros, rows, width)), whole((micros, rows + 16, width))],
+        out_shape=[sds((total, width), BF16)] * 3
+        + [sds((width, total), BF16)]
         + [sds((micros, rows, width), BF16), sds((micros, rows + 16, width), BF16)],
         scratch_shapes=[
             pltpu.VMEM((width, 3 * width), BF16),
             pltpu.VMEM((per, 3 * width), F32),
             pltpu.VMEM((per, PAIR), F32),
             pltpu.VMEM((per, PAIR), F32),
+            pltpu.VMEM((per, width), BF16),
             pltpu.SemaphoreType.DMA,
         ],
         compiler_params=params(),
@@ -773,8 +984,8 @@
         + [ANY, whole((1, width))]
         + table_specs,
         out_specs=[by_step((per, width))] * 3
-        + [by_step((per, hidden_units)), by_step((per, width)), by_step((per, width))]
-        + [by_step((per, 2 * hidden_units)), by_step((per, width)), by_step((per, width))]
+        + [by_step((per, hidden_units)), by_column((width, per)), by_column((width, per))]
+        + [by_step((per, 2 * hidden_units)), by_column((width, per)), by_step((per, width))]
         + [whole((slots, rows, width))] * 2
         + [whole((micros, rows, width))] * 2
         + [whole((8, width))],
@@ -783,10 +994,10 @@
             sds((total, width), F32),
             sds((total, width), BF16),
             sds((total, hidden_units), BF16),
-            sds((total, width), BF16),
-            sds((total, width), BF16),
+            sds((width, total), BF16),
+            sds((width, total), BF16),
             sds((total, 2 * hidden_units), BF16),
-            sds((total, width), BF16),
+            sds((width, total), BF16),
             sds((total, width), BF16),
             sds((slots, rows, width), F32),
             sds((slots, rows, width), F32),
@@ -795,6 +1006,9 @@
             sds((8, width), F32),
         ],
         scratch_shapes=[
+            pltpu.VMEM((per, width), BF16),
+            pltpu.VMEM((per, width), BF16),
+            pltpu.VMEM((per, width), BF16),
             pltpu.VMEM((width, width), BF16),
             pltpu.VMEM((width, 2 * hidden_units), BF16),
             pltpu.VMEM((width, hidden_units), BF16),
@@ -820,41 +1034,46 @@
         q, k.reshape(slots, rows, width), v.reshape(slots, rows, width),
         from_prev, from_next, x, cot, w_all, gain_mid, *tables,
     )
-    result, mid_grad, dq, hid, ffn_grad, normed_two, exp_grad, attended, attn_grad = outs[:9]
+    result, mid_grad, dq, hid, ffn_grad_t, normed_two_t, exp_grad, attended_t, attn_grad = outs[:9]
     dk, dv, back_prev, back_next, mid_term = outs[9:]
 
-    ret_next = shifted(back_prev, "fsdp", -1)
-    ret_prev = shifted(back_next, "fsdp", 1)
-    term_expand = tn(normed_two, exp_grad).astype(BF16)
-    term_contract = tn(ffn_grad, hid).astype(BF16)
-    term_proj = tn(attended, attn_grad).astype(BF16)
-
-    delta, input_grad, pre_term = pl.pallas_call(
-        functools.partial(input_kernel, blocks, group, rows, width),
-        grid=(steps,),
-        in_specs=[SMEM] * 2
-        + [by_step((per, width)), by_step((STEP_SLOTS, rows, width)), by_step((STEP_SLOTS, rows, width))]
-        + [whole((micros, rows, width))] * 2
-        + [by_step((per, width))] * 2
-        + [ANY, whole((1, width))]
-        + table_specs,
-        out_specs=[by_step((per, 3 * width)), by_step((per, width)), whole((8, width))],
-        out_shape=[sds((total, 3 * width), BF16), sds((total, width), BF16), sds((8, width), F32)],
-        scratch_shapes=[
-            pltpu.VMEM((width, 3 * width), BF16),
-            pltpu.VMEM((per, width), F32),
-            pltpu.SemaphoreType.DMA,
-        ],
-        compiler_params=params(),
-        name="input",
-    )(lengths, dealing, dq, dk, dv, ret_next, ret_prev, x, mid_grad, w_all, gain_pre, *tables)
-    term_qkv = tn(normed_one, delta).astype(BF16)
-
-    terms = jnp.stack([jnp.sum(pre_term, axis=0), jnp.sum(mid_term, axis=0)], axis=1)
-    terms = jnp.pad(terms, ((0, 0), (0, PAIR - 2))).astype(BF16)
-    grads = jnp.concatenate([term_qkv, term_expand, term_contract, term_proj, terms], axis=1)
-    at = np.cumsum([0, 3 * width, 2 * hidden_units, hidden_units, width, PAIR]).tolist()
-    qkv_sum, expand_sum, contract_sum, proj_sum, gain_sum = reduce_scatter(grads, share, list(zip(at, at[1:])))
+    at = np.cumsum([0, 2 * hidden_units, hidden_units, width, 3 * width, PAIR]).tolist()
+    cuts = list(zip(at, at[1:]))
+    nz, fs = lax.axis_size("dp"), lax.axis_size("fsdp")
+    if fs == 8 and share % 8 == 0 and nz % 2 == 0:
+        input_grad, expand_sum, contract_sum, proj_sum, qkv_sum, gain_sum = tail(
+            cuts, blocks, group, rows, share, lengths, dealing, gain_pre, tables, mid_term, back_prev, back_next,
+            dq, dk, dv, x, mid_grad, w_all,
+            normed_one_t, normed_two_t, ffn_grad_t, attended_t, exp_grad, hid, attn_grad,
+        )
+    else:
+        ret_next = shifted(back_prev, "fsdp", -1)
+        ret_prev = shifted(back_next, "fsdp", 1)
+        delta, input_grad, pre_term = pl.pallas_call(
+            functools.partial(input_kernel, blocks, group, rows, width),
+            grid=(steps,),
+            in_specs=[SMEM] * 2
+            + [by_step((per, width)), by_step((STEP_SLOTS, rows, width)), by_step((STEP_SLOTS, rows, width))]
+            + [whole((micros, rows, width))] * 2
+            + [by_step((per, width))] * 2
+            + [ANY, whole((1, width))]
+            + table_specs,
+            out_specs=[by_step((per, 3 * width)), by_step((per, width)), whole((8, width))],
+            out_shape=[sds((total, 3 * width), BF16), sds((total, width), BF16), sds((8, width), F32)],
+            scratch_shapes=[
+                pltpu.VMEM((width, 3 * width), BF16),
+                pltpu.VMEM((per, width), F32),
+                pltpu.SemaphoreType.DMA,
+            ],
+            compiler_params=params(),
+            name="input",
+        )(lengths, dealing, dq, dk, dv, ret_next, ret_prev, x, mid_grad, w_all, gain_pre, *tables)
+        terms = jnp.stack([jnp.sum(pre_term, axis=0), jnp.sum(mid_term, axis=0)], axis=1)
+        terms = jnp.pad(terms, ((0, 0), (0, PAIR - 2)))
+        grads = [nn(normed_two_t, exp_grad), nn(ffn_grad_t, hid), nn(attended_t, attn_grad), nn(normed_one_t, delta), terms]
+        grads = jnp.concatenate([g.astype(BF16) for g in grads], axis=1)
+        block = lax.psum_scatter(grads, ("dp", "fsdp"), scatter_dimension=0, tiled=True).astype(F32)
+        expand_sum, contract_sum, proj_sum, qkv_sum, gain_sum = [block[:, begin:end] for begin, end in cuts]
     return (
         result.reshape(inputs.shape),
         input_grad.reshape(inputs.shape),

time: 320 us -> 289 us (0.903)
  matrix products: 22.4 us -> 0 us
  starting transfers between devices: 14.2 us -> 4.53 us
  Pallas kernels: 263 us -> 271 us
    dot_general x4 -> x0, matrix products: 22.4 us -> none  [tn(): lax.dot_general(a, b, (((0,), (0,)), ((), ())), preferred_element_type=F32)]
    ppermute x4 -> x2, starting transfers between devices: 14.2 us -> 4.53 us  [shifted(): return lax.ppermute(block, axis, route)]
    pallas_call x2 -> x1, Pallas kernels: 88.5 us -> 96.4 us  [tail(): pl.pallas_call(functools.partial(tail_kernel, cuts, blocks, group, rows),...]
    unnamed x27 -> x17, local copies, waits for them, and re-layouts: 8.16 us -> 6.58 us
  transfers between devices with their start and end apart: 4 -> 2, of which waited for: 2 -> 1; matrix products, arithmetic and copies ran while one was open for 0% -> 0% of each run, Pallas kernels for 0% -> 0%
where the time goes in v4:
time: 289 us
  Pallas kernels  271 us (94%)
  local copies, waits for them, and re-layouts  10.4 us (4%)
  starting transfers between devices  4.53 us (2%)
    pallas_call x1, Pallas kernels, tail(): pl.pallas_call(functools.partial(tail_kernel, cuts, blocks, group, rows),...  96.4 us
    pallas_call x1, Pallas kernels, local(): pl.pallas_call(functools.partial(layer_kernel, blocks, group, rows, width...  85.7 us
    pallas_call x1, Pallas kernels, gather(): pl.pallas_call(functools.partial(gather_kernel, len(pieces)), in_specs=[p...  63.8 us
    pallas_call x1, Pallas kernels, local(): pl.pallas_call(functools.partial(qkv_kernel, blocks, group, rows, width),...  25 us
    unnamed x17, local copies, waits for them, and re-layouts  6.58 us
  transfers between devices with their start and end apart: 2, of which 1 were waited for; matrix products, arithmetic and copies ran while one was open for 0% of the time, Pallas kernels for 0%

profile of v4, /device:TPU:0, one launch (start us, length us, event | category | flops | bytes accessed | tf_op | source)
XLA Modules:
  0.0 288.7 jit_solution(887532337693911572)
XLA Ops:
  0.6 0.7 pad_maximum_fusion
  1.3 0.1 copy.34
  1.4 0.6 pad.4.refs_4_
  2.0 63.8 %gather.1 = bf16[32,24,6656]{2,1,0:T(8,128)(2,1)} custom-call(bf16[24,2304]{1,0:T(8,128)(2,1)} %refs_0_.1, bf16[24,2304]{1,0:T(8,128)(2,1)} %refs_1_.1, bf16[24,1152]{1,0:T(8,128)(2,1)} %bitcast.27, bf16[24,768]{1,0:T(8,128)(2,1)} %refs_3_.1, bf16[24,128]{1,0:T(8,128)(2,1)} %pad.4.refs_4_), custom_call_target="tpu_custom_call" | custom-call | tf_op jit(solution)/shard_map/gather/pallas_call | solution.py:594
  65.8 1.0 convert_bitcast_fusion
  66.8 0.2 fusion
  67.0 0.7 copy.35.gain
  67.7 25.0 %qkv.1 = (bf16[1280,768]{1,0:T(8,128)(2,1)}, bf16[1280,768]{1,0:T(8,128)(2,1)}, bf16[1280,768]{1,0:T(8,128)(2,1)}, bf16[768,1280]{1,0:T(8,128)(2,1)}, bf16[2,128...) custom-call(s32[2,8]{1,0:T(2,128)} %bitcast.28, s32[2,5]{1,0:T(2,128)} %dealing.5, s32[2,5]{1,0:T(2,128)} %counts.3, ...), custom_call_target="tpu_custom_call" | custom-call | tf_op jit(solution)/shard_map/qkv/pallas_call | solution.py:953
  92.7 1.3 collective-permute-start.1
  94.0 3.2 %collective-permute-start = (bf16[2,128,768]{2,1,0:T(8,128)(2,1)}, bf16[2,128,768]{2,1,0:T(8,128)(2,1)S(1)}, u32[]{:S(2)}, u32[]{:S(2)}) collective-permute-start(bf16[2,128,768]{2,1,0:T(8,128)(2,1)} %get-tuple-element.37), channel_id=1, source_target_pairs={{0,1},{1,2},{2,3},{3,4},{4,5},{5,6},{6,7},{8,9},{9,10},{10,11},{11... | collective-permute-start | bytes 1179656 | tf_op jit(solution)/shard_map/ppermute | solution.py:451
  97.2 0.7 copy.36.gain
  98.0 0.6 collective-permute-done.from_prev
  98.6 0.0 copy-start.1
  98.6 0.0 collective-permute-done.1.from_next
  98.6 0.0 copy-start
  98.6 0.7 copy-done.1
  99.3 0.2 copy-done
  99.5 85.7 %layer.1 = (bf16[1280,768]{1,0:T(8,128)(2,1)}, f32[1280,768]{1,0:T(8,128)}, bf16[1280,768]{1,0:T(8,128)(2,1)}, bf16[1280,1152]{1,0:T(8,128)(2,1)}, bf16[768,1280...) custom-call(s32[2,8]{1,0:T(2,128)} %bitcast.29, ...), custom_call_target="tpu_custom_call" | custom-call | tf_op jit(solution)/shard_map/layer/pallas_call | solution.py:977
  185.2 96.4 %tail.1 = (bf16[1280,768]{1,0:T(8,128)(2,1)}, f32[24,2304]{1,0:T(8,128)}, f32[24,1152]{1,0:T(8,128)}, f32[24,768]{1,0:T(8,128)}, f32[24,2304]{1,0:T(8,128)}, /*index=5*/f32[24,128]{1,0:T(8,128)}) custom-call(s32[2,8]{1,0:T(2,128)} %bitcast.30, s32[2,5]{1,0:T(2,128)} %dealing.5, f32[1,768]{1,0:T(1,128)} %copy.35.gain, f32[40,128]{1,0:T(8,128)} %constant.11.clone.ca, ...), custom_call_target="tpu_custom_call" | custom-call | tf_op jit(solution)/shard_map/tail/pallas_call | solution.py:901
  281.5 1.5 slice_reduce_fusion
  283.0 0.0 copy-start.3
  283.0 0.0 copy-start.5
  283.0 0.0 copy-start.2
  283.0 0.0 copy-start.4
  283.0 3.0 %copy.43 = bf16[2,640,768]{2,1,0:T(8,128)(2,1)} copy(bf16[2,640,768]{2,1,0:T(8,128)(2,1)} %bitcast.25) | data formatting | bytes 3932160
  286.0 0.0 copy-done.3
  286.0 0.7 copy.44
  286.7 0.0 copy-done.5
  286.7 0.6 copy.45
  287.4 0.0 copy-done.2
  287.4 0.7 copy.46
  288.0 0.0 copy-done.4
  288.0 0.6 copy.47
Async XLA Ops:
  92.7 5.9 %collective-permute-start.1 = (bf16[2,144,768]{2,1,0:T(8,128)(2,1)}, bf16[2,144,768]{2,1,0:T(8,128)(2,1)S(1)}, u32[]{:S(2)}, u32[]{:S(2)}) collective-permute-start(bf16[2,144,768]{2,1,0:T(8,128)(2,1)} %get-tuple-element.38), channel_id=1, source_target_pairs={{1,0},{2,1},{3,2},{4,3},{5,4},{6,5},{7,6},{9,8},{10,9},{11,10},{12... | collective-permute-start | bytes 1327112 | tf_op jit(solution)/shard_map/ppermute | solution.py:451
  94.0 4.6 %collective-permute-start = (bf16[2,128,768]{2,1,0:T(8,128)(2,1)}, bf16[2,128,768]{2,1,0:T(8,128)(2,1)S(1)}, u32[]{:S(2)}, u32[]{:S(2)}) collective-permute-start(bf16[2,128,768]{2,1,0:T(8,128)(2,1)} %get-tuple-element.37), channel_id=1, source_target_pairs={{0,1},{1,2},{2,3},{3,4},{4,5},{5,6},{6,7},{8,9},{9,10},{10,11},{11... | collective-permute-start | bytes 1179656 | tf_op jit(solution)/shard_map/ppermute | solution.py:451
  98.6 0.8 copy-start.1
  98.6 0.9 copy-start
  283.0 3.0 %copy-start.3 = (f32[24,2304]{1,0:T(8,128)S(1)}, f32[24,2304]{1,0:T(8,128)}, u32[]{:S(2)}) copy-start(f32[24,2304]{1,0:T(8,128)} %get-tuple-element.74) | copy-start | bytes 663556
  283.0 3.7 %copy-start.5 = (f32[24,768]{1,0:T(8,128)S(1)}, f32[24,768]{1,0:T(8,128)}, u32[]{:S(2)}) copy-start(f32[24,768]{1,0:T(8,128)} %get-tuple-element.75) | copy-start | bytes 221188
  283.0 4.3 %copy-start.2 = (f32[24,2304]{1,0:T(8,128)S(1)}, f32[24,2304]{1,0:T(8,128)}, u32[]{:S(2)}) copy-start(f32[24,2304]{1,0:T(8,128)} %get-tuple-element.76) | copy-start | bytes 663556
  283.0 5.0 %copy-start.4 = (f32[24,1152]{1,0:T(8,128)S(1)}, f32[24,1152]{1,0:T(8,128)}, u32[]{:S(2)}) copy-start(f32[24,1152]{1,0:T(8,128)} %get-tuple-element.58) | copy-start | bytes 331780
